TPU v7x, 32 devices: a whole 2x2x4 slice. The times are simulated.
32 devices in a mesh: lat: 4 (over z), lon: 8 (over y, x, core).
Axes of the slice: x: 2, y: 2, z: 4, core: 2. Of those that a mesh axis runs over, the one named last changes fastest.
Arguments:
- tracers: float32 [16, 8, 64, 1024], P(None, None, 'lat', 'lon'), may hold values from -6 to 6
- winds: float32 [3, 8, 64, 1024], P(None, None, 'lat', 'lon'), may hold values from -4 to 4
- depart_first: int32 [3, 8, 64, 1024], P(None, None, 'lat', 'lon'), may hold values from -3 to 2, as said below
- depart_second: int32 [3, 8, 64, 1024], P(None, None, 'lat', 'lon'), may hold values from -2 to 1, as said below
- fluxes: bfloat16 [384, 128, 256], P(('lat', 'lon')), may hold values from 0.049804688 to 5
- remap_weights: bfloat16 [384, 4, 256, 128], P(('lat', 'lon')), may hold values from 0.00019931793 to 0.019897461
- target_device: int32 [384, 4], P(('lat', 'lon')), may hold values from 0 to 31, all different within a row; in each aligned block of 12 rows (0 to 11, 12 to 23, ...) at most 2 rows name the same one
- target_block: int32 [384, 4], P(('lat', 'lon')), may hold values from 0 to 15
Outputs:
- advected: float32 [16, 8, 64, 1024], P(None, None, 'lat', 'lon')
Inputs may be any that keep to these rules, and one draw needn't show every extreme that they name: `depart_first`: component 0 (levels) is -1 or 0; components 1 and 2 are row and column offsets. `depart_second`: component 0 (levels) is -1 or 0; components 1 and 2 are row and column offsets. `target_device`: device g is the one at lat index g // 8 and lon index g % 8. Each row names 4 different devices; among the rows of one device no device is named more than 2 times.
All inputs are finite; a program needn't handle non-finite values.
Results may differ from a plain program's by a relative error of at most 0.00088.
Values may be sent and summed in bfloat16 or wider, within the bound.
A program may use at most 192 MiB of HBM per device.

v0:
```python
import functools

import jax
import jax.numpy as jnp
from jax import lax
from jax.experimental import pallas as pl
from jax.experimental.pallas import tpu as pltpu
from jax.sharding import PartitionSpec as P

NTR = 16
CAP = 2
BLK_DEV = 16
HMAX = 3


def padded_2(block, sides, width, periodic):
    for axis, dim in sides:
        count = lax.axis_size(axis)
        forward = [(i, i + 1) for i in range(count - 1)]
        if periodic:
            forward.append((count - 1, 0))
        backward = [(target, source) for source, target in forward]
        low = lax.ppermute(
            lax.slice_in_dim(block, block.shape[dim] - width, None, axis=dim), axis, forward
        )
        high = lax.ppermute(lax.slice_in_dim(block, 0, width, axis=dim), axis, backward)
        block = jnp.concatenate([low, block, high], axis=dim)
    return block


def cubic_weights(frac):
    first = -frac * (frac - 1.0) * (frac - 2.0) / 6.0
    second = (frac + 1.0) * (frac - 1.0) * (frac - 2.0) / 2.0
    third = -(frac + 1.0) * frac * (frac - 2.0) / 2.0
    fourth = (frac + 1.0) * frac * (frac - 1.0) / 6.0
    return (first, second, third, fourth)


def level_weights(offset, frac):
    s0, s1, s2, s3 = cubic_weights(frac)
    down = offset < 0
    zero = jnp.zeros_like(frac)
    return [
        jnp.where(down, s0, zero),
        jnp.where(down, s1, s0),
        jnp.where(down, s2, s1),
        jnp.where(down, s3, s2),
        jnp.where(down, zero, s3),
    ]


def offset_weights(offset, frac, reach):
    stencil = cubic_weights(frac)
    spread = []
    for target in range(-reach, reach + 1):
        weight = jnp.zeros(frac.shape, jnp.float32)
        for step in range(4):
            weight = jnp.where(offset == target - step + 1, stencil[step], weight)
        spread.append(weight)
    return spread


def advect_kernel(
    wide, narrow, winds_ref, first_ref, second_ref, wpad_ref, main_ref, halo_ref, out_ref,
    shifted, lhs, rhs, mid_ref, lev_w, row_w, col_w, col_at
):
    levels, height, chans, lanes = main_ref.shape
    comps, rows = winds_ref.shape[0], winds_ref.shape[1]
    taps, reach = 2 * wide + 1, 2 * narrow + 1

    def shift_row(r, carry):
        for comp in range(comps):
            row = wpad_ref[comp, r]
            for e in range(taps):
                piece = row[:, e : e + lanes]
                low, high = piece[:1], piece[levels - 1 :]
                shifted[e * 5 + 0, comp, r] = jnp.concatenate([low, low, piece[: levels - 2]], axis=0)
                shifted[e * 5 + 1, comp, r] = jnp.concatenate([low, piece[: levels - 1]], axis=0)
                shifted[e * 5 + 2, comp, r] = piece
                shifted[e * 5 + 3, comp, r] = jnp.concatenate([piece[1:], high], axis=0)
                shifted[e * 5 + 4, comp, r] = jnp.concatenate([piece[2:], high, high], axis=0)
        return carry

    lax.fori_loop(0, wpad_ref.shape[1], shift_row, 0)

    def wind_row(i, carry):
        wind = [winds_ref[comp, i] for comp in range(comps)]
        off = [first_ref[comp, i] for comp in range(comps)]
        frac = [
            jnp.clip(-wind[comp] - off[comp].astype(jnp.float32), 0.0, 1.0) for comp in range(comps)
        ]
        lw = level_weights(off[0], frac[0])
        rw = offset_weights(off[1], frac[1], wide)
        cw = offset_weights(off[2], frac[2], wide)
        total = [jnp.zeros((levels, lanes), jnp.float32) for comp in range(comps)]
        for across in range(taps):
            for above in range(5):
                pair = lw[above] * rw[across]
                for comp in range(comps):
                    inner = cw[0] * shifted[above, comp, i + across]
                    for e in range(1, taps):
                        inner = inner + cw[e] * shifted[e * 5 + above, comp, i + across]
                    total[comp] = total[comp] + pair * inner
        off = [second_ref[comp, i] for comp in range(comps)]
        frac = [
            jnp.clip(
                -(wind[comp] + total[comp]) * 0.5 - off[comp].astype(jnp.float32), 0.0, 1.0
            )
            for comp in range(comps)
        ]
        for n, weight in enumerate(level_weights(off[0], frac[0])):
            lev_w[n, i] = weight
        for n, weight in enumerate(offset_weights(off[1], frac[1], narrow)):
            row_w[n, i] = weight
        for n, weight in enumerate(cubic_weights(frac[2])):
            col_w[n, i] = weight
        col_at[i] = off[2] - 1 + lax.broadcasted_iota(jnp.int32, (levels, lanes), 1)
        return carry

    lax.fori_loop(0, rows, wind_row, 0)

    lane = lax.broadcasted_iota(jnp.int32, (chans, lanes), 1)
    is_low = jnp.logical_and(lane >= 8, lane < 16)

    def split_row(r, carry):
        for level in range(levels + 4):
            at = min(max(level - 2, 0), levels - 1)
            value = main_ref[at, r]
            top = value.astype(jnp.bfloat16)
            rest = (value - top.astype(jnp.float32)).astype(jnp.bfloat16)
            edge = halo_ref[at, r]
            edge_top = edge.astype(jnp.bfloat16).astype(jnp.float32)
            edge = jnp.where(is_low, edge - edge_top, edge_top).astype(jnp.bfloat16)
            lhs[level, r, :, 0:lanes] = top
            lhs[level, r, :, lanes : 2 * lanes] = rest
            lhs[level, r, :, 2 * lanes : 3 * lanes] = top
            lhs[level, r, :, 3 * lanes : 4 * lanes] = edge
        return carry

    lax.fori_loop(0, height, split_row, 0)

    rhs[...] = jnp.zeros_like(rhs)
    inside = lax.broadcasted_iota(jnp.int32, (lanes, lanes), 0)
    spot = lax.broadcasted_iota(jnp.int32, (8, lanes), 0)
    outside = jnp.where(spot < 4, spot - 4, spot + (lanes - 4))

    def step(t, carry):
        level, first_row = t // (rows // 2), (t % (rows // 2)) * 2
        for side in range(2):
            i = first_row + side
            at = col_at[i, pl.ds(level, 1), :]
            weights = [col_w[n, i, pl.ds(level, 1), :] for n in range(4)]
            cols = slice(side * lanes, (side + 1) * lanes)

            def spread(where):
                away = where - at
                value = jnp.where(away == 0, weights[0], 0.0)
                for n in range(1, 4):
                    value = jnp.where(away == n, weights[n], value)
                top = value.astype(jnp.bfloat16).astype(jnp.float32)
                return top, value - top

            top, rest = spread(inside)
            top16 = top.astype(jnp.bfloat16)
            rhs[0:lanes, cols] = top16
            rhs[lanes : 2 * lanes, cols] = top16
            rhs[2 * lanes : 3 * lanes, cols] = rest.astype(jnp.bfloat16)
            top, rest = spread(outside)
            rhs[3 * lanes : 3 * lanes + 32, cols] = jnp.concatenate(
                [top, top, rest, jnp.zeros_like(rest)], axis=0
            ).astype(jnp.bfloat16)
        span = reach + 1
        left = lhs[pl.ds(level, 5), pl.ds(first_row, span)].reshape(5 * span * chans, 4 * lanes)
        done = jnp.dot(left, rhs[...], preferred_element_type=jnp.float32)
        for side in range(2):
            i = first_row + side
            cols = slice(side * lanes, (side + 1) * lanes)
            rw = [row_w[n, i, pl.ds(level, 1), :] for n in range(reach)]
            total = jnp.zeros((chans, lanes), jnp.float32)
            for above in range(5):
                lw = lev_w[above, i, pl.ds(level, 1), :]
                inner = jnp.zeros((chans, lanes), jnp.float32)
                for n in range(reach):
                    start = (above * span + n + side) * chans
                    inner = inner + rw[n] * done[start : start + chans, cols]
                total = total + lw * inner
            out_ref[level, i] = total
        return carry

    lax.fori_loop(0, levels * (rows // 2), step, 0)


def advect(winds, depart_first, depart_second, wind_wide, tracer_wide, wide, narrow):
    chans, levels, height, _ = tracer_wide.shape
    comps, _, rows, lanes = winds.shape
    by_row = lambda array: array.transpose(0, 2, 1, 3)
    turned = tracer_wide.transpose(1, 2, 0, 3)
    main = turned[..., narrow : narrow + lanes]
    edge = jnp.concatenate([turned[..., :narrow], turned[..., narrow + lanes :]], axis=3)
    gap = jnp.zeros(edge.shape[:3] + (4 - narrow,), jnp.float32)
    edge = jnp.concatenate([gap, edge, gap], axis=3)
    halo = jnp.concatenate(
        [edge, edge, edge, jnp.zeros(edge.shape[:3] + (lanes - 24,), jnp.float32)], axis=3
    )
    vmem = pl.BlockSpec(memory_space=pltpu.VMEM)
    moved = pl.pallas_call(
        functools.partial(advect_kernel, wide, narrow),
        out_shape=jax.ShapeDtypeStruct((levels, rows, chans, lanes), jnp.float32),
        in_specs=[vmem] * 6,
        out_specs=vmem,
        scratch_shapes=[
            pltpu.VMEM((5 * (2 * wide + 1), comps, rows + 2 * wide, levels, lanes), jnp.float32),
            pltpu.VMEM((levels + 4, height, chans, 4 * lanes), jnp.bfloat16),
            pltpu.VMEM((4 * lanes, 2 * lanes), jnp.bfloat16),
            pltpu.VMEM((comps, rows, levels, lanes), jnp.float32),
            pltpu.VMEM((5, rows, levels, lanes), jnp.float32),
            pltpu.VMEM((2 * narrow + 1, rows, levels, lanes), jnp.float32),
            pltpu.VMEM((4, rows, levels, lanes), jnp.float32),
            pltpu.VMEM((rows, levels, lanes), jnp.int32),
        ],
        compiler_params=pltpu.CompilerParams(vmem_limit_bytes=48 * 1024 * 1024),
        cost_estimate=pl.CostEstimate(flops=10**10, bytes_accessed=10**7, transcendentals=0),
        name="advect",
    )(by_row(winds), by_row(depart_first), by_row(depart_second), by_row(wind_wide), main, halo)
    return moved.transpose(2, 0, 1, 3)


def body(
    tracers, winds, depart_first, depart_second, fluxes, remap_weights, target_device, target_block
):
    wide = HMAX + 1
    narrow = max((HMAX + 1) // 2 + 1, HMAX // 2 + 2)
    wind_side = padded_2(winds, (("lon", 3),), wide, True)
    wind_wide = padded_2(wind_side, (("lat", 2),), wide, False)
    tracer_side = padded_2(tracers, (("lon", 3),), narrow, True)
    tracer_wide = padded_2(tracer_side, (("lat", 2),), narrow, False)
    shape = winds.shape[1:]
    moved = advect(winds, depart_first, depart_second, wind_wide, tracer_wide, wide, narrow)
    tiles, links = target_device.shape
    rows_count, block_cols = (fluxes.shape[1], remap_weights.shape[3])
    items = tiles * links
    remapped = jnp.einsum(
        "trc,tkcb->tkrb", fluxes, remap_weights, preferred_element_type=jnp.float32
    )
    remapped = remapped.astype(jnp.bfloat16).reshape(items, rows_count, block_cols)
    lat_count = lax.axis_size("lat")
    lon_count = lax.axis_size("lon")
    devices = lat_count * lon_count
    slot_count = devices * CAP
    owners = target_device.reshape(items)
    item_iota = lax.broadcasted_iota(jnp.int32, (items, items), 1)
    item_rows = lax.broadcasted_iota(jnp.int32, (items, items), 0)
    earlier = jnp.logical_and(owners[:, None] == owners[None, :], item_iota < item_rows)
    rank = jnp.sum(earlier.astype(jnp.int32), axis=1)
    slot = owners * CAP + rank
    slot_iota = lax.broadcasted_iota(jnp.int32, (slot_count, items), 0)
    hit = slot[None, :] == slot_iota
    present = jnp.any(hit, axis=1)
    source_item = jnp.sum(
        jnp.where(hit, lax.broadcasted_iota(jnp.int32, (slot_count, items), 1), 0), axis=1
    )
    outgoing = jnp.take(remapped, source_item, axis=0)
    outgoing = jnp.where(present[:, None, None], outgoing, jnp.zeros_like(outgoing))
    labels = jnp.where(present, jnp.take(target_block.reshape(items), source_item), -1)
    data = outgoing.reshape(devices, CAP, rows_count, block_cols)
    marks = labels.reshape(devices, CAP)
    arrived, arrived_labels = (
        lax.all_to_all(data, ("lat", "lon"), split_axis=0, concat_axis=0, tiled=True),
        lax.all_to_all(marks, ("lat", "lon"), split_axis=0, concat_axis=0, tiled=True),
    )
    arrived_flat = arrived.reshape(slot_count, rows_count * block_cols)
    block_iota = lax.broadcasted_iota(jnp.int32, (BLK_DEV, slot_count), 0)
    selector = (arrived_labels.reshape(1, slot_count) == block_iota).astype(jnp.bfloat16)
    blocks = jnp.dot(selector, arrived_flat, preferred_element_type=jnp.float32)
    levels, lat_rows, lon_cols = shape
    grid = blocks.reshape(BLK_DEV, NTR, levels, block_cols).transpose(1, 2, 0, 3)
    return moved + grid


def solution(mesh):
    in_specs = (
        P(None, None, "lat", "lon"),
        P(None, None, "lat", "lon"),
        P(None, None, "lat", "lon"),
        P(None, None, "lat", "lon"),
        P(("lat", "lon"), None, None),
        P(("lat", "lon"), None, None, None),
        P(("lat", "lon"), None),
        P(("lat", "lon"), None),
    )
    out_specs = P(None, None, "lat", "lon")
    return jax.shard_map(body, mesh=mesh, in_specs=in_specs, out_specs=out_specs, check_vma=False)
```

profile of v0, /device:TPU:0, one launch (start us, length us, event | category | flops | bytes accessed | tf_op | source)
XLA Modules:
  0.0 168.2 jit_solution(3098959114623376895)
XLA Ops:
  0.0 0.9 copy.69
  1.6 0.8 copy.70
  2.5 0.8 gather_fusion
  3.4 0.6 select_select_fusion.1
  4.0 7.3 %all-to-all-start = ((s32[32,1,2]{2,1,0:T(1,128)}), s32[32,1,2]{2,1,0:T(1,128)S(1)}, u32[]{:S(2)}, u32[]{:S(2)}) async-start(s32[32,1,2]{2,1,0:T(1,128)} %bitcast.8), calls=%async_computation | async-start | bytes 32768 | tf_op jit(solution)/shard_map/all_to_all | solution.py:269
  11.6 3.4 %convolution_convert_fusion = bf16[12,4,128,128]{3,2,1,0:T(8,128)(2,1)} fusion(bf16[12,4,256,128]{3,2,1,0:T(8,128)(2,1)S(1)} %copy-done, bf16[12,128,256]{2,1,0:T(8,128)(2,1)} %param.12), kind=kOutput, calls=%fused_computation.7 | convolution fusion | flops 403439616 | bytes 5505024 | tf_op jit(solution)/shard_map/trc,tkcb->tkrb/dot_general | solution.py:242
  14.9 3.6 %gather_fusion.1 = bf16[64,128,128]{1,2,0:T(8,128)(2,1)} fusion(bf16[48,128,128]{1,2,0:T(8,128)(2,1)} %bitcast.48, s32[1024]{0:T(1024)S(1)} %pad_clamp_fusion), kind=kCustom, calls=%fused_computation.1 | custom fusion | bytes 4194560 | tf_op jit(solution)/shard_map/jit(_take)/gather | solution.py:262
  18.5 4.1 %copy.73 = bf16[64,128,128]{2,1,0:T(8,128)(2,1)} copy(bf16[64,128,128]{1,2,0:T(8,128)(2,1)} %gather_fusion.1) | data formatting | bytes 4194304 | tf_op jit(solution)/shard_map/jit(_take)/gather | solution.py:262
  22.6 3.3 %select_select_fusion = bf16[32,2,128,128]{3,2,1,0:T(8,128)(2,1)} fusion(bf16[32,2,128,128]{3,2,1,0:T(8,128)(2,1)} %bitcast.49, pred[32,2]{1,0:T(8,128)(4,1)S(1)} %compare_and_fusion, pred[32,2]{1,0:T(8,128)(4,1)S(1)} %broadcast_in_dim.50), kind=kLoop, calls=%fused_computation.6 | loop fusion | flops 2097152 | bytes 4194432 | tf_op jit(solution)/shard_map/jit(_where)/select_n | solution.py:263
  25.8 6.0 %all-to-all-start.1 = ((bf16[32,2,128,128]{3,2,1,0:T(8,128)(2,1)}), bf16[32,2,128,128]{3,2,1,0:T(8,128)(2,1)}, u32[]{:S(2)}, u32[]{:S(2)}) async-start(bf16[32,2,128,128]{3,2,1,0:T(8,128)(2,1)} %select_select_fusion), calls=%async_computation.1 | async-start | bytes 4194304 | tf_op jit(solution)/shard_map/all_to_all | solution.py:268
  31.9 0.8 fusion.11
  32.7 2.3 %collective-permute-start.1 = (f32[3,8,16,4]{3,1,2,0:T(8,128)}, f32[3,8,16,4]{3,1,2,0:T(8,128)S(1)}, u32[]{:S(2)}, u32[]{:S(2)}) collective-permute-start(f32[3,8,16,4]{3,1,2,0:T(8,128)} %get-tuple-element.14), channel_id=1, source_target_pairs={{1,0},{2,1},{3,2},{4,3},{5,4},{6,5},{7,6},{0,7},{9,8},{10,9},{11,1... | collective-permute-start | bytes 18440 | tf_op jit(solution)/shard_map/ppermute | solution.py:26
  35.0 1.7 fusion.10
  36.7 2.7 %copy.81 = f32[16,8,16,3]{2,1,3,0:T(8,128)} copy(f32[16,8,16,3]{3,2,1,0:T(8,128)} %get-tuple-element.10) | data formatting | bytes 49152
  39.4 2.6 %collective-permute-start.5 = (f32[16,8,16,3]{2,1,3,0:T(8,128)}, f32[16,8,16,3]{2,1,3,0:T(8,128)}, u32[]{:S(2)}, u32[]{:S(2)}) collective-permute-start(f32[16,8,16,3]{2,1,3,0:T(8,128)} %copy.81), channel_id=1, source_target_pairs={{1,0},{2,1},{3,2},{4,3},{5,4},{6,5},{7,6},{0,7},{9,8},{10,9},{11,1... | collective-permute-start | bytes 73736 | tf_op jit(solution)/shard_map/ppermute | solution.py:26
  42.1 2.7 %copy.80 = f32[16,8,16,3]{2,1,3,0:T(8,128)} copy(f32[16,8,16,3]{3,2,1,0:T(8,128)} %get-tuple-element.9) | data formatting | bytes 49152
  44.8 2.8 %copy.67 = f32[16,8,16,128]{3,0,2,1:T(8,128)} copy(f32[16,8,16,128]{3,2,1,0:T(8,128)} %param.8) | data formatting | bytes 2097152 | tf_op args[0]
  47.6 3.3 %collective-permute-done.1 = f32[3,8,16,4]{3,1,2,0:T(8,128)S(1)} collective-permute-done((f32[3,8,16,4]{3,1,2,0:T(8,128)}, f32[3,8,16,4]{3,1,2,0:T(8,128)S(1)}, u32[]{:S(2)}, u32[]{:S(2)}) %collective-permute-start.1) | collective-permute-done | bytes 6176 | tf_op jit(solution)/shard_map/ppermute | solution.py:26
  50.9 3.7 %collective-permute-done = f32[3,8,16,4]{3,1,2,0:T(8,128)} collective-permute-done((f32[3,8,16,4]{3,1,2,0:T(8,128)}, f32[3,8,16,4]{3,1,2,0:T(8,128)}, u32[]{:S(2)}, u32[]{:S(2)}) %collective-permute-start) | collective-permute-done | bytes 6176 | tf_op jit(solution)/shard_map/ppermute | solution.py:23
  54.6 1.6 pad_maximum_fusion.5
  56.3 1.3 collective-permute-start.3
  57.6 5.2 %collective-permute-start.2 = (f32[3,8,4,136]{3,1,2,0:T(8,128)}, f32[3,8,4,136]{3,1,2,0:T(8,128)}, u32[]{:S(2)}, u32[]{:S(2)}) collective-permute-start(f32[3,8,4,136]{3,1,2,0:T(8,128)} %get-tuple-element.11), channel_id=1, source_target_pairs={{0,8},{8,16},{16,24},{1,9},{9,17},{17,25},{2,10},{10,18},{18,26},{... | collective-permute-start | bytes 156680 | tf_op jit(solution)/shard_map/ppermute | solution.py:23
  62.7 2.7 %copy.68 = f32[16,8,16,3]{3,0,2,1:T(8,128)} copy(f32[16,8,16,3]{2,1,3,0:T(8,128)} %collective-permute-done.5) | data formatting | bytes 49152 | tf_op jit(solution)/shard_map/ppermute | solution.py:26
  65.5 2.7 %copy.66 = f32[16,8,16,3]{3,0,2,1:T(8,128)} copy(f32[16,8,16,3]{2,1,3,0:T(8,128)} %collective-permute-done.4) | data formatting | bytes 49152 | tf_op jit(solution)/shard_map/ppermute | solution.py:23
  68.2 2.6 %pad_maximum_fusion.2 = (f32[16,8,3,134]{3,0,2,1:T(8,128)}, f32[16,8,3,134]{3,0,2,1:T(8,128)}) fusion(f32[16,8,16,3]{3,0,2,1:T(8,128)} %copy.68, f32[16,8,16,128]{3,0,2,1:T(8,128)} %copy.67, f32[16,8,16,3]{3,0,2,1:T(8,128)} %copy.66), kind=kLoop, calls=%fused_computation.13 | loop fusion | flops 205824 | bytes 1509376 | tf_op jit(solution)/shard_map/slice | solution.py:24
  70.9 1.3 collective-permute-start.7
  72.1 5.3 %collective-permute-start.6 = (f32[16,8,3,134]{3,0,2,1:T(8,128)}, f32[16,8,3,134]{3,0,2,1:T(8,128)}, u32[]{:S(2)}, u32[]{:S(2)}) collective-permute-start(f32[16,8,3,134]{3,0,2,1:T(8,128)} %get-tuple-element.5), channel_id=1, source_target_pairs={{0,8},{8,16},{16,24},{1,9},{9,17},{17,25},{2,10},{10,18},{18,26},{... | collective-permute-start | bytes 617480 | tf_op jit(solution)/shard_map/ppermute | solution.py:23
  77.5 0.8 copy_bitcast_fusion
  78.8 1.2 reduce.3
  79.9 0.8 eq.36
  80.8 2.3 %maximum_bitcast_fusion.1.wpad_ref = f32[3,24,8,136]{3,2,1,0:T(8,128)} fusion(f32[3,8,4,136]{3,1,2,0:T(8,128)} %collective-permute-done.3, f32[3,8,16,4]{3,1,2,0:T(8,128)} %copy-done.9, f32[3,8,16,128]{3,1,2,0:T(8,128)S(1)} %copy.93, f32[3,8,16,4]{3,1,2,0:T(8,128)} %collective-permute-done, f32[3,8,4,136]{3,1,2,0:T(8,128)} %collective-permute-done.2), kind=kLoop, calls=%fused_computation.10 | loop fusion | flops 313344 | bytes 626688 | tf_op jit(solution)/shard_map/transpose | solution.py:196
  83.1 3.9 %collective-permute-done.7 = f32[16,8,3,134]{3,0,2,1:T(8,128)} collective-permute-done((f32[16,8,3,134]{3,0,2,1:T(8,128)}, f32[16,8,3,134]{3,0,2,1:T(8,128)}, u32[]{:S(2)}, u32[]{:S(2)}) %collective-permute-start.7) | collective-permute-done | bytes 205856 | tf_op jit(solution)/shard_map/ppermute | solution.py:26
  87.0 2.7 %maximum_bitcast_fusion = f32[8,22,16,134]{3,2,1,0:T(8,128)S(1)} fusion(f32[16,8,3,134]{3,0,2,1:T(8,128)} %collective-permute-done.7, f32[16,8,16,3]{3,0,2,1:T(8,128)} %copy.68, f32[16,8,16,128]{3,0,2,1:T(8,128)S(1)} %copy-done.8, f32[16,8,16,3]{3,0,2,1:T(8,128)} %copy.66, f32[16,8,3,134]{3,0,2,1:T(8,128)} %collective-permute-done.6), kind=kLoop, calls=%fused_computation.2 | loop fusion | flops 1509376 | bytes 3018752 | tf_op jit(solution)/shard_map/transpose | solution.py:197
  89.7 1.6 slice.50.main_ref
  91.2 2.2 %fusion.9 = (f32[8,22,16,3]{3,2,1,0:T(8,128)}, f32[8,22,16,3]{3,2,1,0:T(8,128)}) fusion(f32[8,22,16,134]{3,2,1,0:T(8,128)S(1)} %maximum_bitcast_fusion), kind=kLoop, calls=%fused_computation.37 | loop fusion | bytes 135168 | tf_op jit(solution)/shard_map/slice | solution.py:199
  93.4 1.3 broadcast_in_dim.45
  94.7 1.3 broadcast_in_dim.46
  96.0 15.4 %concatenate.21.halo_ref = f32[8,22,16,128]{3,2,1,0:T(8,128)} concatenate(f32[8,22,16,1]{3,2,1,0:T(8,128)} %broadcast_in_dim.45, f32[8,22,16,3]{3,2,1,0:T(8,128)} %get-tuple-element.8, f32[8,22,16,3]{3,2,1,0:T(8,128)} %get-tuple-element.7, f32[8,22,16,1]{3,2,1,0:T(8,128)} %broadcast_in_dim.45, f32[8,22,16,1]{3,2,1,0:T(8,128)} %broadcast_in_dim.45, ...), dimensions={3} | concatenate | bytes 2883584 | tf_op jit(solution)/shard_map/concatenate | solution.py:202
  111.4 1.4 copy-done.1
  112.8 1.4 copy-done.2
  114.1 1.1 copy-done.5
  115.2 0.9 copy-done.6
  116.1 44.4 %advect.1 = f32[8,16,16,128]{3,2,1,0:T(8,128)S(1)} custom-call(f32[3,16,8,128]{3,2,1,0:T(8,128)S(1)} %bitcast.47, s32[3,16,8,128]{3,2,1,0:T(8,128)S(1)} %copy-done.6, s32[3,16,8,128]{3,2,1,0:T(8,128)S(1)} %get-tuple-element.17.second_ref, f32[3,24,8,136]{3,2,1,0:T(8,128)S(1)} %copy-done.5, f32[8,22,16,128]{3,2,1,0:T(8,128)S(1)} %copy-done.1, ...), custom_call_target="tpu_custom_call" | custom-call | flops 10000000000 | bytes 10000000 | tf_op jit(solution)/shard_map/advect/pallas_call | solution.py:206
  160.5 1.0 copy-done.3
  161.5 3.0 %copy.92 = bf16[8,8,128,128]{3,1,2,0:T(8,128)(2,1)S(1)} copy(bf16[8,8,128,128]{3,2,1,0:T(8,128)(2,1)} %bitcast.22) | data formatting | bytes 4194304
  165.0 1.2 fusion
  166.3 0.6 bitcast_add_fusion
  166.9 1.3 copy.76
  (47 shorter events, 2.3 us)
Async XLA Ops:
  0.0 11.6 %copy-start = (bf16[12,4,256,128]{3,2,1,0:T(8,128)(2,1)S(1)}, bf16[12,4,256,128]{3,2,1,0:T(8,128)(2,1)}, u32[]{:S(2)}) copy-start(bf16[12,4,256,128]{3,2,1,0:T(8,128)(2,1)} %param.13) | copy-start | bytes 9437188
  4.0 21.8 %all-to-all-start = ((s32[32,1,2]{2,1,0:T(1,128)}), s32[32,1,2]{2,1,0:T(1,128)S(1)}, u32[]{:S(2)}, u32[]{:S(2)}) async-start(s32[32,1,2]{2,1,0:T(1,128)} %bitcast.8), calls=%async_computation | async-start | bytes 32768 | tf_op jit(solution)/shard_map/all_to_all | solution.py:269
  25.8 6.0 %copy-start.10 = (f32[3,8,16,128]{3,2,1,0:T(8,128)S(1)}, f32[3,8,16,128]{3,2,1,0:T(8,128)}, u32[]{:S(2)}) copy-start(f32[3,8,16,128]{3,2,1,0:T(8,128)} %param.9) | copy-start | bytes 589828
  25.8 135.6 %all-to-all-start.1 = ((bf16[32,2,128,128]{3,2,1,0:T(8,128)(2,1)}), bf16[32,2,128,128]{3,2,1,0:T(8,128)(2,1)}, u32[]{:S(2)}, u32[]{:S(2)}) async-start(bf16[32,2,128,128]{3,2,1,0:T(8,128)(2,1)} %select_select_fusion), calls=%async_computation.1 | async-start | bytes 4194304 | tf_op jit(solution)/shard_map/all_to_all | solution.py:268
  31.8 3.2 %copy-start.7 = (f32[16,8,16,128]{3,2,1,0:T(8,128)S(1)}, f32[16,8,16,128]{3,2,1,0:T(8,128)}, u32[]{:S(2)}) copy-start(f32[16,8,16,128]{3,2,1,0:T(8,128)} %param.8) | copy-start | bytes 3145732
  32.7 18.2 %collective-permute-start.1 = (f32[3,8,16,4]{3,1,2,0:T(8,128)}, f32[3,8,16,4]{3,1,2,0:T(8,128)S(1)}, u32[]{:S(2)}, u32[]{:S(2)}) collective-permute-start(f32[3,8,16,4]{3,1,2,0:T(8,128)} %get-tuple-element.14), channel_id=1, source_target_pairs={{1,0},{2,1},{3,2},{4,3},{5,4},{6,5},{7,6},{0,7},{9,8},{10,9},{11,1... | collective-permute-start | bytes 18440 | tf_op jit(solution)/shard_map/ppermute | solution.py:26
  35.0 19.6 %collective-permute-start = (f32[3,8,16,4]{3,1,2,0:T(8,128)}, f32[3,8,16,4]{3,1,2,0:T(8,128)}, u32[]{:S(2)}, u32[]{:S(2)}) collective-permute-start(f32[3,8,16,4]{3,1,2,0:T(8,128)} %get-tuple-element.13), channel_id=1, source_target_pairs={{0,1},{1,2},{2,3},{3,4},{4,5},{5,6},{6,7},{7,0},{8,9},{9,10},{10,1... | collective-permute-start | bytes 18440 | tf_op jit(solution)/shard_map/ppermute | solution.py:23
  39.4 23.3 %collective-permute-start.5 = (f32[16,8,16,3]{2,1,3,0:T(8,128)}, f32[16,8,16,3]{2,1,3,0:T(8,128)}, u32[]{:S(2)}, u32[]{:S(2)}) collective-permute-start(f32[16,8,16,3]{2,1,3,0:T(8,128)} %copy.81), channel_id=1, source_target_pairs={{1,0},{2,1},{3,2},{4,3},{5,4},{6,5},{7,6},{0,7},{9,8},{10,9},{11,1... | collective-permute-start | bytes 73736 | tf_op jit(solution)/shard_map/ppermute | solution.py:26
  44.8 20.7 %collective-permute-start.4 = (f32[16,8,16,3]{2,1,3,0:T(8,128)}, f32[16,8,16,3]{2,1,3,0:T(8,128)}, u32[]{:S(2)}, u32[]{:S(2)}) collective-permute-start(f32[16,8,16,3]{2,1,3,0:T(8,128)} %copy.80), channel_id=1, source_target_pairs={{0,1},{1,2},{2,3},{3,4},{4,5},{5,6},{6,7},{7,0},{8,9},{9,10},{10,1... | collective-permute-start | bytes 73736 | tf_op jit(solution)/shard_map/ppermute | solution.py:23
  50.9 19.9 %copy-start.9 = (f32[3,8,16,4]{3,1,2,0:T(8,128)}, f32[3,8,16,4]{3,1,2,0:T(8,128)S(1)}, u32[]{:S(2)}) copy-start(f32[3,8,16,4]{3,1,2,0:T(8,128)S(1)} %collective-permute-done.1) | copy-start | bytes 18436
  56.3 24.5 %collective-permute-start.3 = (f32[3,8,4,136]{3,1,2,0:T(8,128)}, f32[3,8,4,136]{3,1,2,0:T(8,128)}, u32[]{:S(2)}, u32[]{:S(2)}) collective-permute-start(f32[3,8,4,136]{3,1,2,0:T(8,128)} %get-tuple-element.12), channel_id=1, source_target_pairs={{8,0},{16,8},{24,16},{9,1},{17,9},{25,17},{10,2},{18,10},{26,18},{... | collective-permute-start | bytes 156680 | tf_op jit(solution)/shard_map/ppermute | solution.py:26
  57.6 23.2 %collective-permute-start.2 = (f32[3,8,4,136]{3,1,2,0:T(8,128)}, f32[3,8,4,136]{3,1,2,0:T(8,128)}, u32[]{:S(2)}, u32[]{:S(2)}) collective-permute-start(f32[3,8,4,136]{3,1,2,0:T(8,128)} %get-tuple-element.11), channel_id=1, source_target_pairs={{0,8},{8,16},{16,24},{1,9},{9,17},{17,25},{2,10},{10,18},{18,26},{... | collective-permute-start | bytes 156680 | tf_op jit(solution)/shard_map/ppermute | solution.py:23
  68.2 9.3 %copy-start.11 = (s32[3,8,16,128]{3,2,1,0:T(8,128)S(1)}, s32[3,8,16,128]{3,2,1,0:T(8,128)}, u32[]{:S(2)}) copy-start(s32[3,8,16,128]{3,2,1,0:T(8,128)} %param.11) | copy-start | bytes 589828
  68.2 9.3 %copy-start.12 = (s32[3,8,16,128]{3,2,1,0:T(8,128)S(1)}, s32[3,8,16,128]{3,2,1,0:T(8,128)}, u32[]{:S(2)}) copy-start(s32[3,8,16,128]{3,2,1,0:T(8,128)} %param.10) | copy-start | bytes 589828
  70.9 16.1 %collective-permute-start.7 = (f32[16,8,3,134]{3,0,2,1:T(8,128)}, f32[16,8,3,134]{3,0,2,1:T(8,128)}, u32[]{:S(2)}, u32[]{:S(2)}) collective-permute-start(f32[16,8,3,134]{3,0,2,1:T(8,128)} %get-tuple-element.6), channel_id=1, source_target_pairs={{8,0},{16,8},{24,16},{9,1},{17,9},{25,17},{10,2},{18,10},{26,18},{... | collective-permute-start | bytes 617480 | tf_op jit(solution)/shard_map/ppermute | solution.py:26
  72.1 14.8 %collective-permute-start.6 = (f32[16,8,3,134]{3,0,2,1:T(8,128)}, f32[16,8,3,134]{3,0,2,1:T(8,128)}, u32[]{:S(2)}, u32[]{:S(2)}) collective-permute-start(f32[16,8,3,134]{3,0,2,1:T(8,128)} %get-tuple-element.5), channel_id=1, source_target_pairs={{0,8},{8,16},{16,24},{1,9},{9,17},{17,25},{2,10},{10,18},{18,26},{... | collective-permute-start | bytes 617480 | tf_op jit(solution)/shard_map/ppermute | solution.py:23
  80.8 6.2 %copy-start.8 = (f32[16,8,16,128]{3,0,2,1:T(8,128)S(1)}, f32[16,8,16,128]{3,0,2,1:T(8,128)}, u32[]{:S(2)}) copy-start(f32[16,8,16,128]{3,0,2,1:T(8,128)} %copy.67) | copy-start | bytes 3145732
  111.4 1.4 copy-start.1
  112.8 1.4 copy-start.2
  114.1 1.1 copy-start.5
  115.2 0.9 copy-start.6
  160.5 1.0 copy-start.3
  165.0 1.2 copy-start.4
where the time goes:
time: 171 us; the launch traced here: 168 us
  local copies, waits for them, and re-layouts  61.4 us (36%)
  Pallas kernels  44.4 us (26%)
  starting transfers between devices  31.3 us (18%)
  other arithmetic  15.3 us (9%)
  waiting for transfers between devices  10.9 us (6%)
  matrix products  4.62 us (3%)
    pallas_call x1, Pallas kernels, advect(): pl.pallas_call(functools.partial(advect_kernel, wide, narrow), out_shape=...  44.4 us
    unnamed x34, local copies, waits for them, and re-layouts  19.3 us
    concatenate x1, local copies, waits for them, and re-layouts, advect(): jnp.concatenate([edge, edge, edge, jnp.zeros(edge.shape[:3] + (lanes - 24...  15.4 us
    ppermute x4, starting transfers between devices, padded_2(): lax.ppermute(lax.slice_in_dim(block, block.shape[dim] - width, None, axis...  10.5 us
    gather x2, local copies, waits for them, and re-layouts, body(): outgoing = jnp.take(remapped, source_item, axis=0)  7.62 us
    ppermute x4, starting transfers between devices, padded_2(): lax.ppermute(lax.slice_in_dim(block, 0, width, axis=dim), axis, backward)  7.52 us
    all_to_all x1, starting transfers between devices, body(): lax.all_to_all(marks, ('lat', 'lon'), split_axis=0, concat_axis=0, tiled=...  7.33 us
    ppermute x4, waiting for transfers between devices, padded_2(): lax.ppermute(lax.slice_in_dim(block, 0, width, axis=dim), axis, backward)  7.23 us
  transfers between devices with their start and end apart: 10, of which 3 were waited for; matrix products, arithmetic and copies ran while one was open for 39% of the time, Pallas kernels for 26%

commit v1 on v0

v1 whole, which is shorter than its diff:
```python
import functools

import jax
import jax.numpy as jnp
from jax import lax
from jax.experimental import pallas as pl
from jax.experimental.pallas import tpu as pltpu
from jax.sharding import PartitionSpec as P

CAP = 2
HMAX = 3
MESH = pl.DeviceIdType.MESH
LANES = 128
BIG = 1 << 20


def cubic_weights(frac):
    first = -frac * (frac - 1.0) * (frac - 2.0) / 6.0
    second = (frac + 1.0) * (frac - 1.0) * (frac - 2.0) / 2.0
    third = -(frac + 1.0) * frac * (frac - 2.0) / 2.0
    fourth = (frac + 1.0) * frac * (frac - 1.0) / 6.0
    return (first, second, third, fourth)


def level_weights(offset, frac):
    s0, s1, s2, s3 = cubic_weights(frac)
    down = offset < 0
    zero = jnp.zeros_like(frac)
    return [
        jnp.where(down, s0, zero),
        jnp.where(down, s1, s0),
        jnp.where(down, s2, s1),
        jnp.where(down, s3, s2),
        jnp.where(down, zero, s3),
    ]


def offset_weights(offset, frac, reach):
    stencil = cubic_weights(frac)
    spread = []
    for target in range(-reach, reach + 1):
        weight = jnp.zeros(frac.shape, jnp.float32)
        for step in range(4):
            weight = jnp.where(offset == target - step + 1, stencil[step], weight)
        spread.append(weight)
    return spread


def step_kernel(
    dims,
    winds_hbm, first_hbm, second_hbm, tracers_hbm, fluxes_hbm, weights_hbm, owner_ref, block_ref,
    moved_ref, arrived_ref, labels_ref,
    winds_v, first_v, second_v, tracers_v, fluxes_v, weights_v,
    outgoing, codes_v, codes_s, marks_v,
    wind_pack, wind_rows, tracer_pack, tracer_rows,
    wind_side, wind_diag, wind_far, tracer_side, tracer_diag, tracer_far,
    shifted, lhs, rhs_a, rhs_b, masks, lev_w, row_w, col_w, col_at,
    load_sem, code_sem, halo_send, halo_recv, item_send, item_recv, mark_send, mark_recv,
):
    chans, levels, rows, comps, tiles, links, blocks, wide, narrow = dims
    lanes = LANES
    plane = levels * rows
    taps, reach = 2 * wide + 1, 2 * narrow + 1
    lat, lon = lax.axis_index("lat"), lax.axis_index("lon")
    lat_count, lon_count = lax.axis_size("lat"), lax.axis_size("lon")
    devices = lat_count * lon_count
    me = lat * lon_count + lon

    loads = [
        pltpu.make_async_copy(source, target, load_sem.at[n])
        for n, (source, target) in enumerate(
            (
                (winds_hbm, winds_v),
                (tracers_hbm, tracers_v),
                (fluxes_hbm, fluxes_v),
                (weights_hbm, weights_v),
                (first_hbm, first_v),
                (second_hbm, second_v),
            )
        )
    ]
    for load in loads:
        load.start()

    barrier = pltpu.get_barrier_semaphore()

    def greet(k, carry):
        p = lax.rem(me + k, devices)
        pl.semaphore_signal(
            barrier, inc=1, device_id=(p // lon_count, lax.rem(p, lon_count)), device_id_type=MESH
        )
        return carry

    lax.fori_loop(1, devices, greet, 0)

    width = codes_v.shape[1]
    spot = lax.broadcasted_iota(jnp.int32, (1, width), 1)
    lowest = jnp.full((1, width), BIG, jnp.int32)
    highest = jnp.full((1, width), -1, jnp.int32)
    for t in range(tiles):
        for k in range(links):
            code = (t * links + k) * blocks + block_ref[t, k]
            hit = spot == owner_ref[t, k]
            lowest = jnp.minimum(lowest, jnp.where(hit, code, BIG))
            highest = jnp.maximum(highest, jnp.where(hit, code, -1))
    used = highest >= 0
    twice = highest != lowest
    low_code = jnp.where(used, lowest, 0)
    high_code = jnp.where(used, highest, 0)
    codes_v[...] = jnp.concatenate([low_code // blocks, high_code // blocks], axis=0)
    marks_v[...] = jnp.concatenate(
        [
            jnp.where(used, low_code % blocks, -1),
            jnp.where(jnp.logical_and(used, twice), high_code % blocks, -1),
        ],
        axis=0,
    )
    code_copy = pltpu.make_async_copy(codes_v, codes_s, code_sem)
    code_copy.start()

    lane8 = lax.broadcasted_iota(jnp.int32, (8, lanes), 1)
    lane16 = lax.broadcasted_iota(jnp.int32, (chans, lanes), 1)

    def wind_main(ref, comp, i):
        return ref[pl.ds(comp * plane + i, levels, stride=rows), :]

    def tracer_main(level, r):
        return tracers_v[pl.ds(level * rows + r, chans, stride=plane), :]

    loads[0].wait()
    for half in range(rows // 8):
        for comp in range(comps):
            packed = jnp.zeros((levels, lanes), jnp.float32)
            for p in range(8):
                value = wind_main(winds_v, comp, half * 8 + p)
                packed = jnp.where(
                    lane8 // 16 == p, pltpu.roll(value, (16 * p + 8) % lanes, 1), packed
                )
            wind_pack[half, comp] = packed
    for comp in range(comps):
        for r in range(wide):
            wind_rows[0, comp, r] = wind_main(winds_v, comp, r)
            wind_rows[1, comp, r] = wind_main(winds_v, comp, rows - wide + r)
    loads[1].wait()

    def pack_row(r, carry):
        packed = jnp.zeros((chans, lanes), jnp.float32)
        for level in range(levels):
            value = tracer_main(level, r)
            packed = jnp.where(
                lane16 // 16 == level, pltpu.roll(value, (16 * level + 8) % lanes, 1), packed
            )
        tracer_pack[r] = packed
        return carry

    lax.fori_loop(0, rows, pack_row, 0)
    for r in range(narrow):
        for level in range(levels):
            tracer_rows[0, r, level] = tracer_main(level, r)
            tracer_rows[1, r, level] = tracer_main(level, rows - narrow + r)

    pl.semaphore_wait(barrier, devices - 1)

    west, east = lax.rem(lon + lon_count - 1, lon_count), lax.rem(lon + 1, lon_count)
    north, south = lat - 1, lat + 1

    def halo(n, source, target, where):
        return pltpu.make_async_remote_copy(
            src_ref=source, dst_ref=target, send_sem=halo_send.at[n], recv_sem=halo_recv.at[n],
            device_id=where, device_id_type=MESH,
        )

    def side_copies(base, pack, side):
        return [halo(base, pack, side.at[0], (lat, east)), halo(base + 1, pack, side.at[1], (lat, west))]

    def north_copies(base, cut, whole, diag, far):
        return [
            halo(base, cut, diag.at[1, 0], (north, east)),
            halo(base + 1, cut, diag.at[1, 1], (north, west)),
            halo(base + 2, whole, far.at[1], (north, lon)),
        ]

    def south_copies(base, cut, whole, diag, far):
        return [
            halo(base, cut, diag.at[0, 0], (south, east)),
            halo(base + 1, cut, diag.at[0, 1], (south, west)),
            halo(base + 2, whole, far.at[0], (south, lon)),
        ]

    wind_sides = side_copies(0, wind_pack, wind_side)
    wind_north = north_copies(2, wind_pack.at[0], wind_rows.at[0], wind_diag, wind_far)
    wind_south = south_copies(5, wind_pack.at[rows // 8 - 1], wind_rows.at[1], wind_diag, wind_far)
    tracer_sides = side_copies(8, tracer_pack, tracer_side)
    tracer_north = north_copies(
        10, tracer_pack.at[pl.ds(0, narrow)], tracer_rows.at[0], tracer_diag, tracer_far
    )
    tracer_south = south_copies(
        13, tracer_pack.at[pl.ds(rows - narrow, narrow)], tracer_rows.at[1], tracer_diag, tracer_far
    )
    has_north, has_south = lat > 0, lat < lat_count - 1

    for copy in wind_sides:
        copy.start()

    @pl.when(has_north)
    def _():
        for copy in wind_north:
            copy.start()

    @pl.when(has_south)
    def _():
        for copy in wind_south:
            copy.start()

    @pl.when(has_north)
    def _():
        for copy in tracer_north:
            copy.start()

    @pl.when(has_south)
    def _():
        for copy in tracer_south:
            copy.start()

    for copy in tracer_sides:
        copy.start()

    code_copy.wait()
    loads[2].wait()
    loads[3].wait()

    def item_copy(p):
        return pltpu.make_async_remote_copy(
            src_ref=outgoing.at[p], dst_ref=arrived_ref.at[me],
            send_sem=item_send.at[p], recv_sem=item_recv.at[me],
            device_id=(p // lon_count, lax.rem(p, lon_count)), device_id_type=MESH,
        )

    def mark_copy(p):
        return pltpu.make_async_remote_copy(
            src_ref=marks_v, dst_ref=labels_ref.at[me],
            send_sem=mark_send.at[p], recv_sem=mark_recv.at[me],
            device_id=(p // lon_count, lax.rem(p, lon_count)), device_id_type=MESH,
        )

    def product(p, c):
        item = codes_s[c, p]
        return jnp.dot(
            fluxes_v[item // links], weights_v[item], preferred_element_type=jnp.float32
        ).astype(jnp.bfloat16)

    middle = lat_count // 2
    order = sorted(range(lat_count), key=lambda away: abs(2 * away - lat_count) * 2 + (away > middle))
    order = [(away, side) for away in order for side in range(lon_count) if away or side]
    total_peers = devices - 1

    def peer_at(n):
        away = n // lon_count
        step = (away + 1) // 2
        signed = jnp.where(away % 2 == 1, -step, step)
        there = lax.rem(lat + middle + signed + lat_count, lat_count)
        return there, lax.rem(lon + n + 1, lon_count)

    def emit(n, carry):
        there, side = peer_at(n)
        p = there * lon_count + side
        for c in range(CAP):
            outgoing[p, c] = product(p, c)

        @pl.when(n > 0)
        def _():
            before, beside = peer_at(n - 1)
            item_copy(before * lon_count + beside).start()

        mark_copy(p).start()
        return carry

    lax.fori_loop(0, total_peers, emit, 0)
    there, side = peer_at(total_peers - 1)
    for c in range(CAP):
        arrived_ref[me, c] = product(me, c)
    labels_ref[me] = marks_v[...]
    item_copy(there * lon_count + side).start()

    loads[4].wait()
    loads[5].wait()
    for copy in wind_sides:
        copy.wait_recv()

    @pl.when(has_north)
    def _():
        for copy in wind_south:
            copy.wait_recv()

    @pl.when(has_south)
    def _():
        for copy in wind_north:
            copy.wait_recv()

    from_west = lane8 % 16 < 8

    def put_shifts(comp, r, main, edge):
        for e in range(taps):
            d = e - wide
            if d > 0:
                piece = pltpu.roll(jnp.where(lane8 < d, edge, main), lanes - d, 1)
            elif d < 0:
                piece = pltpu.roll(jnp.where(lane8 >= lanes + d, edge, main), -d, 1)
            else:
                piece = main
            low, high = piece[:1], piece[levels - 1 :]
            shifted[e * 5 + 0, comp, r] = jnp.concatenate([low, low, piece[: levels - 2]], axis=0)
            shifted[e * 5 + 1, comp, r] = jnp.concatenate([low, piece[: levels - 1]], axis=0)
            shifted[e * 5 + 2, comp, r] = piece
            shifted[e * 5 + 3, comp, r] = jnp.concatenate([piece[1:], high], axis=0)
            shifted[e * 5 + 4, comp, r] = jnp.concatenate([piece[2:], high, high], axis=0)

    for half in range(rows // 8):
        for comp in range(comps):
            def shift_row(p, carry, half=half, comp=comp):
                merged = jnp.where(from_west, wind_side[0, half, comp], wind_side[1, half, comp])
                edge = pltpu.roll(merged, lax.rem(2 * lanes - 8 - 16 * p, lanes), 1)
                put_shifts(comp, wide + half * 8 + p, wind_main(winds_v, comp, half * 8 + p), edge)
                return carry

            lax.fori_loop(0, 8, shift_row, 0)

    def far_rows(place, present, start, first_row):
        for comp in range(comps):
            def far_row(r, carry, comp=comp):
                merged = jnp.where(from_west, wind_diag[place, 0, comp], wind_diag[place, 1, comp])
                edge = pltpu.roll(merged, lax.rem(2 * lanes - 8 - 16 * (first_row + r), lanes), 1)
                main = wind_far[place, comp, r]
                edge = jnp.where(present, edge, 0.0)
                main = jnp.where(present, main, 0.0)
                put_shifts(comp, start + r, main, edge)
                return carry

            lax.fori_loop(0, wide, far_row, 0)

    far_rows(0, has_north, 0, 8 - wide)
    far_rows(1, has_south, wide + rows, 0)

    column = lax.broadcasted_iota(jnp.int32, (levels, lanes), 1)

    def wind_row(i, carry):
        wind = [wind_main(winds_v, comp, i) for comp in range(comps)]
        off = [wind_main(first_v, comp, i) for comp in range(comps)]
        frac = [
            jnp.clip(-wind[comp] - off[comp].astype(jnp.float32), 0.0, 1.0) for comp in range(comps)
        ]
        lw = level_weights(off[0], frac[0])
        rw = offset_weights(off[1], frac[1], wide)
        cw = offset_weights(off[2], frac[2], wide)
        total = [jnp.zeros((levels, lanes), jnp.float32) for comp in range(comps)]
        for across in range(taps):
            for above in range(5):
                pair = lw[above] * rw[across]
                for comp in range(comps):
                    inner = cw[0] * shifted[above, comp, i + across]
                    for e in range(1, taps):
                        inner = inner + cw[e] * shifted[e * 5 + above, comp, i + across]
                    total[comp] = total[comp] + pair * inner
        off = [wind_main(second_v, comp, i) for comp in range(comps)]
        frac = [
            jnp.clip(
                -(wind[comp] + total[comp]) * 0.5 - off[comp].astype(jnp.float32), 0.0, 1.0
            )
            for comp in range(comps)
        ]
        for n, weight in enumerate(level_weights(off[0], frac[0])):
            lev_w[n, i] = weight
        for n, weight in enumerate(offset_weights(off[1], frac[1], narrow)):
            row_w[n, i] = weight
        for n, weight in enumerate(cubic_weights(frac[2])):
            col_w[n, i] = weight
        col_at[i] = off[2] - 1 + column
        return carry

    lax.fori_loop(0, rows, wind_row, 0)

    for copy in tracer_sides:
        copy.wait_recv()

    @pl.when(has_north)
    def _():
        for copy in tracer_south:
            copy.wait_recv()

    @pl.when(has_south)
    def _():
        for copy in tracer_north:
            copy.wait_recv()

    from_west16 = lane16 % 16 < 8

    def put_split(r, merged, main):
        turned = [merged] + [
            pltpu.roll(merged, lanes - 16 * s, 1) for s in range(1, levels)
        ]
        for level in range(levels):
            value = main(level)
            top = value.astype(jnp.bfloat16)
            lhs[level, r, :, 0:lanes] = top
            lhs[level, r, :, lanes : 2 * lanes] = (value - top.astype(jnp.float32)).astype(jnp.bfloat16)
            edge = jnp.where(
                lane16 < 16,
                turned[level],
                jnp.where(lane16 < 32, turned[(level - 1) % levels], turned[(level - 2) % levels]),
            )
            edge_top = edge.astype(jnp.bfloat16).astype(jnp.float32)
            edge = jnp.where(lane16 < 32, edge_top, edge - edge_top)
            lhs[level, r, :, 2 * lanes : 3 * lanes] = edge.astype(jnp.bfloat16)

    def split_row(r, carry):
        merged = jnp.where(from_west16, tracer_side[0, r], tracer_side[1, r])
        put_split(narrow + r, merged, lambda level: tracer_main(level, r))
        return carry

    lax.fori_loop(0, rows, split_row, 0)

    def split_far(place, present, start):
        def far_row(r, carry):
            merged = jnp.where(from_west16, tracer_diag[place, 0, r], tracer_diag[place, 1, r])
            merged = jnp.where(present, merged, 0.0)
            put_split(
                start + r, merged, lambda level: jnp.where(present, tracer_far[place, r, level], 0.0)
            )
            return carry

        lax.fori_loop(0, narrow, far_row, 0)

    split_far(0, has_north, 0)
    split_far(1, has_south, narrow + rows)

    deep, across16 = (
        lax.broadcasted_iota(jnp.int32, (16, lanes), 0),
        lax.broadcasted_iota(jnp.int32, (16, lanes), 1),
    )
    groups = lanes // 16
    for t in range(groups):
        near = jnp.abs(16 * t + deep - across16) <= narrow
        masks[t] = jnp.where(near, 1.0, 0.0).astype(jnp.bfloat16)
    outer = jnp.where(deep < 8, deep - 8, deep + (lanes - 8))
    masks[groups] = jnp.where(jnp.abs(outer - across16) <= narrow, 1.0, 0.0).astype(jnp.bfloat16)
    rhs_a[...] = jnp.zeros_like(rhs_a)
    rhs_b[...] = jnp.zeros_like(rhs_b)
    deep8 = lax.broadcasted_iota(jnp.int32, (8, lanes), 0)

    def build(level, pair, rhs):
        for side in range(2):
            i = pair * 2 + side
            cols = slice(side * lanes, (side + 1) * lanes)
            at = col_at[i, pl.ds(level, 1), :]
            away = jnp.bitwise_and(deep8 - at, 7)
            value = jnp.zeros((8, lanes), jnp.float32)
            for n in range(4):
                value = jnp.where(away == n, col_w[n, i, pl.ds(level, 1), :], value)
            rest = value - value.astype(jnp.bfloat16).astype(jnp.float32)
            top16 = jnp.concatenate([value, value], axis=0).astype(jnp.bfloat16)
            rest16 = jnp.concatenate([rest, rest], axis=0).astype(jnp.bfloat16)
            for t in range(groups):
                top = top16 * masks[t]
                rhs[16 * t : 16 * t + 16, cols] = top
                rhs[2 * lanes + 16 * t : 2 * lanes + 16 * t + 16, cols] = top
                rhs[lanes + 16 * t : lanes + 16 * t + 16, cols] = rest16 * masks[t]
            top = top16 * masks[groups]
            rhs[3 * lanes : 3 * lanes + 16, cols] = top
            rhs[3 * lanes + 16 : 3 * lanes + 32, cols] = rest16 * masks[groups]
            rhs[3 * lanes + 32 : 3 * lanes + 48, cols] = top

    span = reach + 1

    def apply(level, pair, rhs):
        low, high = max(level - 2, 0), min(level + 2, levels - 1)
        count = high - low + 1
        part = lambda at: lhs[low : high + 1, pl.ds(pair * 2, span), :, at * lanes : (at + 1) * lanes].reshape(
            count * span * chans, lanes
        )
        top, rest, edge = part(0), part(1), part(2)
        left = jnp.concatenate([top, top, rest, edge], axis=1)
        done = jnp.dot(left, rhs[...], preferred_element_type=jnp.float32)
        for side in range(2):
            i = pair * 2 + side
            cols = slice(side * lanes, (side + 1) * lanes)
            rw = [row_w[n, i, pl.ds(level, 1), :] for n in range(reach)]
            total = jnp.zeros((chans, lanes), jnp.float32)
            for m in range(count):
                lw = None
                for n in range(5):
                    if min(max(level - 2 + n, 0), levels - 1) == low + m:
                        weight = lev_w[n, i, pl.ds(level, 1), :]
                        lw = weight if lw is None else lw + weight
                inner = jnp.zeros((chans, lanes), jnp.float32)
                for n in range(reach):
                    start = (m * span + n + side) * chans
                    inner = inner + rw[n] * done[start : start + chans, cols]
                total = total + lw * inner
            moved_ref[pl.ds(i * chans * levels + level, chans, stride=levels), :] = total

    pairs = rows // 2
    for level in range(levels):
        build(level, 0, rhs_a)

        def both(q, carry, level=level):
            build(level, 2 * q + 1, rhs_b)
            apply(level, 2 * q, rhs_a)
            build(level, jnp.minimum(2 * q + 2, pairs - 1), rhs_a)
            apply(level, 2 * q + 1, rhs_b)
            return carry

        lax.fori_loop(0, pairs // 2, both, 0)

    for copy in wind_sides + tracer_sides:
        copy.wait_send()

    @pl.when(has_north)
    def _():
        for copy in wind_north + tracer_north:
            copy.wait_send()

    @pl.when(has_south)
    def _():
        for copy in wind_south + tracer_south:
            copy.wait_send()

    def finish(n, carry):
        p = lax.rem(me + n, devices)
        where = (p // lon_count, lax.rem(p, lon_count))
        item_copy(p).wait_send()
        mark_copy(p).wait_send()
        pltpu.make_async_remote_copy(
            src_ref=outgoing.at[p], dst_ref=arrived_ref.at[p],
            send_sem=item_send.at[p], recv_sem=item_recv.at[p],
            device_id=where, device_id_type=MESH,
        ).wait_recv()
        pltpu.make_async_remote_copy(
            src_ref=marks_v, dst_ref=labels_ref.at[p],
            send_sem=mark_send.at[p], recv_sem=mark_recv.at[p],
            device_id=where, device_id_type=MESH,
        ).wait_recv()
        return carry

    lax.fori_loop(1, devices, finish, 0)


def join_kernel(dims, moved_ref, arrived_ref, labels_ref, out_ref, total):
    chans, levels, rows, blocks = dims
    me = lax.axis_index("lat") * lax.axis_size("lon") + lax.axis_index("lon")
    depth = chans * levels
    for s in range(rows):
        total[s] = moved_ref[s * depth : (s + 1) * depth, :]

    def add(n, carry):
        for c in range(CAP):
            label = labels_ref[n, c, me]
            at = jnp.where(label < 0, blocks, label)
            total[at] = total[at] + arrived_ref[n, c].astype(jnp.float32)
        return carry

    lax.fori_loop(0, arrived_ref.shape[0], add, 0)
    for s in range(rows):
        for g in range(depth // 8):
            out_ref[pl.ds(g * 8 * rows + s, 8, stride=rows), :] = total[s, g * 8 : g * 8 + 8, :]


def body(
    tracers, winds, depart_first, depart_second, fluxes, remap_weights, target_device, target_block
):
    wide = HMAX + 1
    narrow = max((HMAX + 1) // 2 + 1, HMAX // 2 + 2)
    chans, levels, rows, lanes = tracers.shape
    comps = winds.shape[0]
    tiles, links = target_device.shape
    depth, cells = fluxes.shape[1:]
    cols = remap_weights.shape[3]
    blocks = rows * lanes // cols
    devices = lax.axis_size("lat") * lax.axis_size("lon")
    height = rows + 2 * narrow
    padded = -(-devices // LANES) * LANES
    dims = (chans, levels, rows, comps, tiles, links, blocks, wide, narrow)
    flat = lambda array: array.reshape(-1, lanes)
    hbm = pl.BlockSpec(memory_space=pl.ANY)
    vmem = pl.BlockSpec(memory_space=pltpu.VMEM)
    smem = pl.BlockSpec(memory_space=pltpu.SMEM)
    f32, b16, i32 = jnp.float32, jnp.bfloat16, jnp.int32
    dma = pltpu.SemaphoreType.DMA
    moved, arrived, labels = pl.pallas_call(
        functools.partial(step_kernel, dims),
        out_shape=(
            jax.ShapeDtypeStruct((chans * levels * rows, lanes), f32),
            jax.ShapeDtypeStruct((devices, CAP, depth, cols), b16),
            jax.ShapeDtypeStruct((devices, CAP, padded), i32),
        ),
        in_specs=[hbm] * 6 + [smem] * 2,
        out_specs=(vmem, vmem, vmem),
        scratch_shapes=[
            pltpu.VMEM((comps * levels * rows, lanes), f32),
            pltpu.VMEM((comps * levels * rows, lanes), i32),
            pltpu.VMEM((comps * levels * rows, lanes), i32),
            pltpu.VMEM((chans * levels * rows, lanes), f32),
            pltpu.VMEM((tiles, depth, cells), b16),
            pltpu.VMEM((tiles * links, cells, cols), b16),
            pltpu.VMEM((devices, CAP, depth, cols), b16),
            pltpu.VMEM((CAP, padded), i32),
            pltpu.SMEM((CAP, padded), i32),
            pltpu.VMEM((CAP, padded), i32),
            pltpu.VMEM((rows // 8, comps, levels, lanes), f32),
            pltpu.VMEM((2, comps, wide, levels, lanes), f32),
            pltpu.VMEM((rows, chans, lanes), f32),
            pltpu.VMEM((2, narrow, levels, chans, lanes), f32),
            pltpu.VMEM((2, rows // 8, comps, levels, lanes), f32),
            pltpu.VMEM((2, 2, comps, levels, lanes), f32),
            pltpu.VMEM((2, comps, wide, levels, lanes), f32),
            pltpu.VMEM((2, rows, chans, lanes), f32),
            pltpu.VMEM((2, 2, narrow, chans, lanes), f32),
            pltpu.VMEM((2, narrow, levels, chans, lanes), f32),
            pltpu.VMEM((5 * (2 * wide + 1), comps, rows + 2 * wide, levels, lanes), f32),
            pltpu.VMEM((levels, height, chans, 3 * lanes), b16),
            pltpu.VMEM((4 * lanes, 2 * lanes), b16),
            pltpu.VMEM((4 * lanes, 2 * lanes), b16),
            pltpu.VMEM((lanes // 16 + 1, 16, lanes), b16),
            pltpu.VMEM((5, rows, levels, lanes), f32),
            pltpu.VMEM((2 * narrow + 1, rows, levels, lanes), f32),
            pltpu.VMEM((4, rows, levels, lanes), f32),
            pltpu.VMEM((rows, levels, lanes), i32),
            dma((6,)),
            dma(()),
            dma((16,)),
            dma((16,)),
            dma((devices,)),
            dma((devices,)),
            dma((devices,)),
            dma((devices,)),
        ],
        compiler_params=pltpu.CompilerParams(
            collective_id=0, has_side_effects=True, vmem_limit_bytes=62 * 1024 * 1024
        ),
        name="step",
    )(
        flat(winds), flat(depart_first), flat(depart_second), flat(tracers), fluxes,
        remap_weights.reshape(tiles * links, cells, cols), target_device, target_block,
    )
    out = pl.pallas_call(
        functools.partial(join_kernel, (chans, levels, rows, blocks)),
        out_shape=jax.ShapeDtypeStruct((chans * levels * rows, lanes), f32),
        in_specs=[vmem, vmem, smem],
        out_specs=vmem,
        scratch_shapes=[pltpu.VMEM((blocks + 1, chans * levels, lanes), f32)],
        name="join",
    )(moved, arrived, labels)
    return out.reshape(chans, levels, rows, lanes)


def solution(mesh):
    in_specs = (
        P(None, None, "lat", "lon"),
        P(None, None, "lat", "lon"),
        P(None, None, "lat", "lon"),
        P(None, None, "lat", "lon"),
        P(("lat", "lon"), None, None),
        P(("lat", "lon"), None, None, None),
        P(("lat", "lon"), None),
        P(("lat", "lon"), None),
    )
    out_specs = P(None, None, "lat", "lon")
    return jax.shard_map(body, mesh=mesh, in_specs=in_specs, out_specs=out_specs, check_vma=False)
```

time: 171 us -> 70.5 us (0.41)
  the two profiles are of different devices: /device:TPU:0 before, /device:TPU:8 now
where the time goes in v1:
time: 70.5 us; the launch traced here: 70.2 us
  Pallas kernels  67.5 us (96%)
  local copies, waits for them, and re-layouts  2.72 us (4%)
    pallas_call x1, Pallas kernels, body(): pl.pallas_call(functools.partial(step_kernel, dims), out_shape=(jax.Shape...  63.3 us
    pallas_call x1, Pallas kernels, body(): pl.pallas_call(functools.partial(join_kernel, (chans, levels, rows, block...  4.17 us
    unnamed x2, local copies, waits for them, and re-layouts  2.72 us

profile of v1, /device:TPU:8, one launch (start us, length us, event | category | flops | bytes accessed | tf_op | source)
XLA Modules:
  0.0 70.2 jit_solution(1363786859337653475)
XLA Ops:
  0.0 1.4 %copy.9.owner_ref = s32[12,4]{1,0:T(8,128)} copy(s32[12,4]{0,1:T(4,128)} %param.14) | data formatting | bytes 384 | tf_op args[6]
  1.4 1.4 %copy.10.block_ref = s32[12,4]{1,0:T(8,128)} copy(s32[12,4]{0,1:T(4,128)} %param.15) | data formatting | bytes 384 | tf_op args[7]
  2.7 63.3 %step.1 = (f32[2048,128]{1,0:T(8,128)}, bf16[32,2,128,128]{3,2,1,0:T(8,128)(2,1)}, s32[32,2,128]{2,1,0:T(2,128)}) custom-call(f32[384,128]{1,0:T(8,128)} %bitcast.8, s32[384,128]{1,0:T(8,128)} %bitcast.9, s32[384,128]{1,0:T(8,128)} %bitcast.10, f32[2048,128]{1,0:T(8,128)} %bitcast.7, bf16[12,128,256]{2,1,0:T(8,128)(2,1)} %fluxes_hbm.1, ...), custom_call_target="tpu_custom_call" | custom-call | tf_op jit(solution)/shard_map/step/pallas_call | solution.py:588
  66.0 4.2 %join.1 = f32[2048,128]{1,0:T(8,128)} custom-call(f32[2048,128]{1,0:T(8,128)} %get-tuple-element.8.moved_ref, bf16[32,2,128,128]{3,2,1,0:T(8,128)(2,1)} %get-tuple-element.9.arrived_ref, s32[32,2,128]{2,1,0:T(2,128)} %get-tuple-element.10.labels_ref), custom_call_target="tpu_custom_call" | custom-call | tf_op jit(solution)/shard_map/join/pallas_call | solution.py:644

commit v2 on v1

v2 whole, which is shorter than its diff:
```python
import functools

import jax
import jax.numpy as jnp
from jax import lax
from jax.experimental import pallas as pl
from jax.experimental.pallas import tpu as pltpu
from jax.sharding import PartitionSpec as P

CAP = 2
HMAX = 3
MESH = pl.DeviceIdType.MESH
LANES = 128
BIG = 1 << 20


def cubic_weights(frac):
    first = -frac * (frac - 1.0) * (frac - 2.0) / 6.0
    second = (frac + 1.0) * (frac - 1.0) * (frac - 2.0) / 2.0
    third = -(frac + 1.0) * frac * (frac - 2.0) / 2.0
    fourth = (frac + 1.0) * frac * (frac - 1.0) / 6.0
    return (first, second, third, fourth)


def level_weights(offset, frac):
    s0, s1, s2, s3 = cubic_weights(frac)
    down = offset < 0
    zero = jnp.zeros_like(frac)
    return [
        jnp.where(down, s0, zero),
        jnp.where(down, s1, s0),
        jnp.where(down, s2, s1),
        jnp.where(down, s3, s2),
        jnp.where(down, zero, s3),
    ]


def offset_weights(offset, frac, reach):
    stencil = cubic_weights(frac)
    spread = []
    for target in range(-reach, reach + 1):
        weight = jnp.zeros(frac.shape, jnp.float32)
        for step in range(4):
            weight = jnp.where(offset == target - step + 1, stencil[step], weight)
        spread.append(weight)
    return spread


def step_kernel(
    dims,
    winds_hbm, first_hbm, second_hbm, tracers_hbm, fluxes_hbm, weights_hbm, owner_ref, block_ref,
    moved_ref, arrived_ref, labels_ref,
    wind_pad, first_v, second_v, tracer_pad, fluxes_v, weights_v,
    products, outgoing, codes_v, codes_s, marks_v,
    wind_pack, tracer_pack, wind_edge, tracer_edge,
    shifted, lhs, rhs_a, rhs_b, masks, wind_w, wind_sum, lev_w, row_w, col_w, col_at, moved_v,
    wind_sem, tracer_sem, first_sem, second_sem, load_sem, code_sem, moved_sem,
    halo_send, halo_recv, item_send, item_recv, mark_send, mark_recv,
):
    chans, levels, rows, comps, tiles, links, blocks, wide, narrow = dims
    lanes = LANES
    taps, reach = 2 * wide + 1, 2 * narrow + 1
    lat, lon = lax.axis_index("lat"), lax.axis_index("lon")
    lat_count, lon_count = lax.axis_size("lat"), lax.axis_size("lon")
    devices = lat_count * lon_count
    me = lat * lon_count + lon

    def by_level(source, target, sem, start):
        return [
            pltpu.make_async_copy(
                source.at[:, level], target.at[:, pl.ds(start, rows), level, :], sem.at[level]
            )
            for level in range(levels)
        ]

    wind_loads = by_level(winds_hbm, wind_pad, wind_sem, wide)
    tracer_loads = [
        pltpu.make_async_copy(
            tracers_hbm.at[chan], tracer_pad.at[:, pl.ds(narrow, rows), chan, :], tracer_sem.at[chan]
        )
        for chan in range(chans)
    ]
    flux_load = pltpu.make_async_copy(fluxes_hbm, fluxes_v, load_sem.at[0])
    weight_load = pltpu.make_async_copy(weights_hbm, weights_v, load_sem.at[1])
    late_loads = by_level(first_hbm, first_v, first_sem, 0) + by_level(second_hbm, second_v, second_sem, 0)
    for load in wind_loads + tracer_loads + [flux_load, weight_load] + late_loads:
        load.start()

    barrier = pltpu.get_barrier_semaphore()

    def greet(k, carry):
        p = lax.rem(me + k, devices)
        pl.semaphore_signal(
            barrier, inc=1, device_id=(p // lon_count, lax.rem(p, lon_count)), device_id_type=MESH
        )
        return carry

    lax.fori_loop(1, devices, greet, 0)

    width = codes_v.shape[1]
    spot = lax.broadcasted_iota(jnp.int32, (1, width), 1)
    lowest = jnp.full((1, width), BIG, jnp.int32)
    highest = jnp.full((1, width), -1, jnp.int32)
    for t in range(tiles):
        for k in range(links):
            code = (t * links + k) * blocks + block_ref[k, t]
            hit = spot == owner_ref[k, t]
            lowest = jnp.minimum(lowest, jnp.where(hit, code, BIG))
            highest = jnp.maximum(highest, jnp.where(hit, code, -1))
    used = highest >= 0
    twice = highest != lowest
    low_code = jnp.where(used, lowest, 0)
    high_code = jnp.where(used, highest, 0)
    codes_v[...] = jnp.concatenate([low_code // blocks, high_code // blocks], axis=0)
    marks_v[...] = jnp.concatenate(
        [
            jnp.where(used, low_code % blocks, -1),
            jnp.where(jnp.logical_and(used, twice), high_code % blocks, -1),
        ],
        axis=0,
    )
    code_copy = pltpu.make_async_copy(codes_v, codes_s, code_sem)
    code_copy.start()

    lane8 = lax.broadcasted_iota(jnp.int32, (levels, lanes), 1)
    lane16 = lax.broadcasted_iota(jnp.int32, (chans, lanes), 1)
    west, east = lax.rem(lon + lon_count - 1, lon_count), lax.rem(lon + 1, lon_count)
    north, south = lat - 1, lat + 1
    has_north, has_south = lat > 0, lat < lat_count - 1
    halves = rows // 8

    for load in wind_loads:
        load.wait()
    for half in range(halves):
        for comp in range(comps):
            packed = jnp.zeros((levels, lanes), jnp.float32)
            for p in range(8):
                value = wind_pad[comp, wide + half * 8 + p]
                packed = jnp.where(
                    lane8 // 16 == p, pltpu.roll(value, (16 * p + 8) % lanes, 1), packed
                )
            wind_pack[half, comp] = packed
    for load in tracer_loads:
        load.wait()

    def pack_row(r, carry):
        for side in range(2):
            packed = jnp.zeros((chans, lanes), jnp.float32)
            for level in range(levels):
                value = tracer_pad[level, narrow + 2 * r + side]
                packed = jnp.where(
                    lane16 // 16 == level, pltpu.roll(value, (16 * level + 8) % lanes, 1), packed
                )
            tracer_pack[2 * r + side] = packed
        return carry

    lax.fori_loop(0, rows // 2, pack_row, 0)

    @pl.when(jnp.logical_not(has_north))
    def _():
        wind_pad[:, 0:wide] = jnp.zeros((comps, wide, levels, lanes), jnp.float32)
        wind_edge[:, 0] = jnp.zeros((2, comps, levels, lanes), jnp.float32)
        tracer_pad[:, 0:narrow] = jnp.zeros((levels, narrow, chans, lanes), jnp.float32)
        tracer_edge[:, 0:narrow] = jnp.zeros((2, narrow, chans, lanes), jnp.float32)

    @pl.when(jnp.logical_not(has_south))
    def _():
        wind_pad[:, wide + rows :] = jnp.zeros((comps, wide, levels, lanes), jnp.float32)
        wind_edge[:, halves + 1] = jnp.zeros((2, comps, levels, lanes), jnp.float32)
        tracer_pad[:, narrow + rows :] = jnp.zeros((levels, narrow, chans, lanes), jnp.float32)
        tracer_edge[:, narrow + rows :] = jnp.zeros((2, narrow, chans, lanes), jnp.float32)

    pl.semaphore_wait(barrier, devices - 1)

    def halo(n, source, target, where):
        return pltpu.make_async_remote_copy(
            src_ref=source, dst_ref=target, send_sem=halo_send.at[n], recv_sem=halo_recv.at[n],
            device_id=where, device_id_type=MESH,
        )

    wind_sides = [
        halo(0, wind_pack, wind_edge.at[0, pl.ds(1, halves)], (lat, east)),
        halo(1, wind_pack, wind_edge.at[1, pl.ds(1, halves)], (lat, west)),
    ]
    wind_north = [
        halo(2, wind_pad.at[:, pl.ds(wide, wide)], wind_pad.at[:, pl.ds(wide + rows, wide)], (north, lon)),
        halo(3, wind_pack.at[0], wind_edge.at[0, halves + 1], (north, east)),
        halo(4, wind_pack.at[0], wind_edge.at[1, halves + 1], (north, west)),
    ]
    wind_south = [
        halo(5, wind_pad.at[:, pl.ds(rows, wide)], wind_pad.at[:, pl.ds(0, wide)], (south, lon)),
        halo(6, wind_pack.at[halves - 1], wind_edge.at[0, 0], (south, east)),
        halo(7, wind_pack.at[halves - 1], wind_edge.at[1, 0], (south, west)),
    ]
    first_rows, last_rows = pl.ds(0, narrow), pl.ds(rows - narrow, narrow)
    above_rows, below_rows = pl.ds(0, narrow), pl.ds(narrow + rows, narrow)
    tracer_sides = [
        halo(8, tracer_pack, tracer_edge.at[0, pl.ds(narrow, rows)], (lat, east)),
        halo(9, tracer_pack, tracer_edge.at[1, pl.ds(narrow, rows)], (lat, west)),
    ]
    tracer_north = [
        halo(10, tracer_pad.at[:, pl.ds(narrow, narrow)], tracer_pad.at[:, below_rows], (north, lon)),
        halo(11, tracer_pack.at[first_rows], tracer_edge.at[0, below_rows], (north, east)),
        halo(12, tracer_pack.at[first_rows], tracer_edge.at[1, below_rows], (north, west)),
    ]
    tracer_south = [
        halo(13, tracer_pad.at[:, pl.ds(rows, narrow)], tracer_pad.at[:, above_rows], (south, lon)),
        halo(14, tracer_pack.at[last_rows], tracer_edge.at[0, above_rows], (south, east)),
        halo(15, tracer_pack.at[last_rows], tracer_edge.at[1, above_rows], (south, west)),
    ]

    def each(condition, copies, act):
        @pl.when(condition)
        def _():
            for copy in copies:
                act(copy)

    start, arrive, leave = (lambda c: c.start()), (lambda c: c.wait_recv()), (lambda c: c.wait_send())
    each(has_north, wind_north, start)
    each(has_south, wind_south, start)
    for copy in wind_sides:
        copy.start()
    each(has_north, tracer_north, start)
    each(has_south, tracer_south, start)
    for copy in tracer_sides:
        copy.start()

    code_copy.wait()
    flux_load.wait()
    weight_load.wait()
    group = 3 if tiles % 3 == 0 else 1

    def multiply(n, carry):
        for g in range(group):
            t = n * group + g
            right = jnp.concatenate([weights_v[t, k] for k in range(links)], axis=1)
            done = jnp.dot(fluxes_v[t], right, preferred_element_type=jnp.float32)
            for k in range(links):
                products[t * links + k] = done[:, k * lanes : (k + 1) * lanes].astype(jnp.bfloat16)
        return carry

    lax.fori_loop(0, tiles // group, multiply, 0)

    def item_copy(p):
        return pltpu.make_async_remote_copy(
            src_ref=outgoing.at[p], dst_ref=arrived_ref.at[me],
            send_sem=item_send.at[p], recv_sem=item_recv.at[me],
            device_id=(p // lon_count, lax.rem(p, lon_count)), device_id_type=MESH,
        )

    def mark_copy(p):
        return pltpu.make_async_remote_copy(
            src_ref=marks_v, dst_ref=labels_ref.at[me],
            send_sem=mark_send.at[p], recv_sem=mark_recv.at[me],
            device_id=(p // lon_count, lax.rem(p, lon_count)), device_id_type=MESH,
        )

    middle = lat_count // 2
    away = sorted(range(lat_count), key=lambda n: abs(n - middle))
    last = None

    def peer(there, n):
        return there * lon_count + lax.rem(lon + n, lon_count)

    for far in away:
        there = lax.rem(lat + far, lat_count)

        def emit(n, carry, there=there):
            p = peer(there, n)
            for c in range(CAP):
                outgoing[p, c] = products[codes_s[c, p]]
            before = peer(there, n - 1)

            @pl.when(n > 1)
            def _():
                item_copy(before).start()

            mark_copy(p).start()
            return carry

        if last is not None:
            for c in range(CAP):
                outgoing[peer(there, 0), c] = products[codes_s[c, peer(there, 0)]]
            item_copy(last).start()
            if far:
                item_copy(peer(there, 0)).start()
                mark_copy(peer(there, 0)).start()
        else:
            for c in range(CAP):
                outgoing[peer(there, 0), c] = products[codes_s[c, peer(there, 0)]]
            item_copy(peer(there, 0)).start()
            mark_copy(peer(there, 0)).start()
        lax.fori_loop(1, lon_count, emit, 0)
        last = peer(there, lon_count - 1)
    item_copy(last).start()
    own_items = pltpu.make_async_copy(outgoing.at[me], arrived_ref.at[me], item_recv.at[me])
    own_items.start()
    own_marks = pltpu.make_async_copy(marks_v, labels_ref.at[me], mark_recv.at[me])
    own_marks.start()

    deep, across16 = (
        lax.broadcasted_iota(jnp.int32, (16, lanes), 0),
        lax.broadcasted_iota(jnp.int32, (16, lanes), 1),
    )
    groups = lanes // 16
    for t in range(groups):
        near = jnp.abs(16 * t + deep - across16) <= narrow
        masks[t] = jnp.where(near, 1.0, 0.0).astype(jnp.bfloat16)
    outer = jnp.where(deep < 8, deep - 8, deep + (lanes - 8))
    masks[groups] = jnp.where(jnp.abs(outer - across16) <= narrow, 1.0, 0.0).astype(jnp.bfloat16)
    rhs_a[...] = jnp.zeros_like(rhs_a)
    rhs_b[...] = jnp.zeros_like(rhs_b)

    for load in late_loads:
        load.wait()
    for copy in wind_sides:
        copy.wait_recv()
    each(has_north, wind_south, arrive)
    each(has_south, wind_north, arrive)

    def shift_row(r, carry):
        turned = r + 8 - wide
        half, p = turned // 8, turned % 8
        back = lax.rem(2 * lanes - 8 - 16 * p, lanes)
        for comp in range(comps):
            merged = jnp.where(lane8 % 16 < 8, wind_edge[0, half, comp], wind_edge[1, half, comp])
            edge = pltpu.roll(merged, back, 1)
            main = wind_pad[comp, r]
            for e in range(taps):
                d = e - wide
                if d > 0:
                    piece = pltpu.roll(jnp.where(lane8 < d, edge, main), lanes - d, 1)
                elif d < 0:
                    piece = pltpu.roll(jnp.where(lane8 >= lanes + d, edge, main), -d, 1)
                else:
                    piece = main
                low, high = piece[:1], piece[levels - 1 :]
                shifted[e * 5 + 0, comp, r] = jnp.concatenate([low, low, piece[: levels - 2]], axis=0)
                shifted[e * 5 + 1, comp, r] = jnp.concatenate([low, piece[: levels - 1]], axis=0)
                shifted[e * 5 + 2, comp, r] = piece
                shifted[e * 5 + 3, comp, r] = jnp.concatenate([piece[1:], high], axis=0)
                shifted[e * 5 + 4, comp, r] = jnp.concatenate([piece[2:], high, high], axis=0)
        return carry

    lax.fori_loop(0, rows + 2 * wide, shift_row, 0)

    column = lax.broadcasted_iota(jnp.int32, (levels, lanes), 1)

    def wind_start(side, i):
        off = [first_v[comp, i] for comp in range(comps)]
        frac = [
            jnp.clip(-wind_pad[comp, wide + i] - off[comp].astype(jnp.float32), 0.0, 1.0)
            for comp in range(comps)
        ]
        weights = level_weights(off[0], frac[0])
        weights += offset_weights(off[1], frac[1], wide) + offset_weights(off[2], frac[2], wide)
        for n, weight in enumerate(weights):
            wind_w[side, n] = weight
        for comp in range(comps):
            wind_sum[side, comp] = jnp.zeros((levels, lanes), jnp.float32)

    def wind_unit(first, q):
        sides = [side for side in range(2) if 0 <= q - side < taps]
        cw = [[wind_w[side, 5 + taps + e] for e in range(taps)] for side in sides]
        rw = [wind_w[side, 5 + q - side] for side in sides]
        total = [[wind_sum[side, comp] for comp in range(comps)] for side in sides]
        for above in range(5):
            pair = [wind_w[side, above] * rw[n] for n, side in enumerate(sides)]
            for comp in range(comps):
                inner = [None] * len(sides)
                for e in range(taps):
                    value = shifted[e * 5 + above, comp, first + q]
                    for n in range(len(sides)):
                        term = cw[n][e] * value
                        inner[n] = term if e == 0 else inner[n] + term
                for n in range(len(sides)):
                    total[n][comp] = total[n][comp] + pair[n] * inner[n]
        for n, side in enumerate(sides):
            for comp in range(comps):
                wind_sum[side, comp] = total[n][comp]

    def wind_finish(side, i):
        off = [second_v[comp, i] for comp in range(comps)]
        frac = [
            jnp.clip(
                -(wind_pad[comp, wide + i] + wind_sum[side, comp]) * 0.5
                - off[comp].astype(jnp.float32),
                0.0,
                1.0,
            )
            for comp in range(comps)
        ]
        for n, weight in enumerate(level_weights(off[0], frac[0])):
            lev_w[n, i] = weight
        for n, weight in enumerate(offset_weights(off[1], frac[1], narrow)):
            row_w[n, i] = weight
        for n, weight in enumerate(cubic_weights(frac[2])):
            col_w[n, i] = weight
        col_at[i] = off[2] - 1 + column

    for side in range(2):
        wind_start(side, side)

    wind_unit(0, 0)
    for q in range(1, taps):
        wind_unit(0, q)
    wind_unit(0, taps)
    for side in range(2):
        wind_finish(side, side)

    for copy in tracer_sides:
        copy.wait_recv()
    each(has_north, tracer_south, arrive)
    each(has_south, tracer_north, arrive)

    def split_row(r, carry):
        merged = jnp.where(lane16 % 16 < 8, tracer_edge[0, r], tracer_edge[1, r])
        turned = [merged] + [pltpu.roll(merged, lanes - 16 * s, 1) for s in range(1, levels)]
        for level in range(levels):
            value = tracer_pad[level, r]
            top = value.astype(jnp.bfloat16)
            lhs[level, r, :, 0:lanes] = top
            lhs[level, r, :, lanes : 2 * lanes] = (value - top.astype(jnp.float32)).astype(jnp.bfloat16)
            edge = jnp.where(
                lane16 < 16,
                turned[level],
                jnp.where(lane16 < 32, turned[(level - 1) % levels], turned[(level - 2) % levels]),
            )
            edge_top = edge.astype(jnp.bfloat16).astype(jnp.float32)
            edge = jnp.where(lane16 < 32, edge_top, edge - edge_top)
            lhs[level, r, :, 2 * lanes : 3 * lanes] = edge.astype(jnp.bfloat16)
        return carry

    lax.fori_loop(0, rows + 2 * narrow, split_row, 0)

    deep8 = lax.broadcasted_iota(jnp.int32, (8, lanes), 0)

    def build(level, pair, rhs):
        for side in range(2):
            i = pair * 2 + side
            cols = slice(side * lanes, (side + 1) * lanes)
            at = col_at[i, pl.ds(level, 1), :]
            away = jnp.bitwise_and(deep8 - at, 7)
            value = jnp.zeros((8, lanes), jnp.float32)
            for n in range(4):
                value = jnp.where(away == n, col_w[n, i, pl.ds(level, 1), :], value)
            rest = value - value.astype(jnp.bfloat16).astype(jnp.float32)
            top16 = jnp.concatenate([value, value], axis=0).astype(jnp.bfloat16)
            rest16 = jnp.concatenate([rest, rest], axis=0).astype(jnp.bfloat16)
            for t in range(groups):
                top = top16 * masks[t]
                rhs[16 * t : 16 * t + 16, cols] = top
                rhs[2 * lanes + 16 * t : 2 * lanes + 16 * t + 16, cols] = top
                rhs[lanes + 16 * t : lanes + 16 * t + 16, cols] = rest16 * masks[t]
            top = top16 * masks[groups]
            rhs[3 * lanes : 3 * lanes + 16, cols] = top
            rhs[3 * lanes + 16 : 3 * lanes + 32, cols] = rest16 * masks[groups]
            rhs[3 * lanes + 32 : 3 * lanes + 48, cols] = top

    span = reach + 1

    def apply(level, pair, rhs):
        low, high = max(level - 2, 0), min(level + 2, levels - 1)
        count = high - low + 1
        part = lambda at: lhs[
            low : high + 1, pl.ds(pair * 2, span), :, at * lanes : (at + 1) * lanes
        ].reshape(count * span * chans, lanes)
        top, rest, edge = part(0), part(1), part(2)
        left = jnp.concatenate([top, top, rest, edge], axis=1)
        done = jnp.dot(left, rhs[...], preferred_element_type=jnp.float32)
        for side in range(2):
            i = pair * 2 + side
            cols = slice(side * lanes, (side + 1) * lanes)
            rw = [row_w[n, i, pl.ds(level, 1), :] for n in range(reach)]
            total = jnp.zeros((chans, lanes), jnp.float32)
            for m in range(count):
                lw = None
                for n in range(5):
                    if min(max(level - 2 + n, 0), levels - 1) == low + m:
                        weight = lev_w[n, i, pl.ds(level, 1), :]
                        lw = weight if lw is None else lw + weight
                inner = jnp.zeros((chans, lanes), jnp.float32)
                for n in range(reach):
                    first = (m * span + n + side) * chans
                    inner = inner + rw[n] * done[first : first + chans, cols]
                total = total + lw * inner
            moved_v[i, level] = total

    pairs = rows // 2
    shares = levels - 1
    cuts = [(n * (taps + 1) + shares // 2) // shares for n in range(shares + 1)]
    both = [rhs_a, rhs_b]
    build(0, 0, rhs_a)

    def moved_copy(pair):
        return pltpu.make_async_copy(
            moved_v.at[pl.ds(pair * 2, 2)], moved_ref.at[pl.ds(pair * 2, 2)], moved_sem.at[pair]
        )

    def pair_step(pair, carry):
        after = jnp.minimum(pair + 1, pairs - 1)
        def level_step(level):
            if level == 0:
                for side in range(2):
                    wind_start(side, after * 2 + side)
            if level < shares:
                for q in range(cuts[level], cuts[level + 1]):
                    wind_unit(after * 2, q)
            if level == shares - 1:
                for side in range(2):
                    wind_finish(side, after * 2 + side)
            if level < levels - 1:
                build(level + 1, pair, both[(level + 1) % 2])
            else:
                build(0, after, both[0])
            apply(level, pair, both[level % 2])

        for level in range(levels):
            pl.when(pair >= 0)(functools.partial(level_step, level))
        moved_copy(pair).start()
        return carry

    lax.fori_loop(0, pairs, pair_step, 0)
    for pair in range(pairs):
        moved_copy(pair).wait()

    for copy in wind_sides + tracer_sides:
        copy.wait_send()
    each(has_north, wind_north + tracer_north, leave)
    each(has_south, wind_south + tracer_south, leave)
    own_items.wait()
    own_marks.wait()

    def finish(n, carry):
        p = lax.rem(me + n, devices)
        where = (p // lon_count, lax.rem(p, lon_count))
        item_copy(p).wait_send()
        mark_copy(p).wait_send()
        pltpu.make_async_remote_copy(
            src_ref=outgoing.at[p], dst_ref=arrived_ref.at[p],
            send_sem=item_send.at[p], recv_sem=item_recv.at[p],
            device_id=where, device_id_type=MESH,
        ).wait_recv()
        pltpu.make_async_remote_copy(
            src_ref=marks_v, dst_ref=labels_ref.at[p],
            send_sem=mark_send.at[p], recv_sem=mark_recv.at[p],
            device_id=where, device_id_type=MESH,
        ).wait_recv()
        return carry

    lax.fori_loop(1, devices, finish, 0)


def join_kernel(dims, moved_hbm, arrived_hbm, labels_ref, out_hbm, total, more, arrived, moved_sem, item_sem, out_sem):
    chans, levels, rows, blocks, share = dims
    me = lax.axis_index("lat") * lax.axis_size("lon") + lax.axis_index("lon")
    loads = [
        pltpu.make_async_copy(
            moved_hbm.at[:, level], total.at[pl.ds(0, rows), :, level, :], moved_sem.at[level]
        )
        for level in range(levels)
    ]
    for load in loads:
        load.start()
    parts = arrived.shape[0] // share

    def piece(n):
        cut = pl.ds(n * share, share)
        return pltpu.make_async_copy(arrived_hbm.at[cut], arrived.at[cut], item_sem.at[n])

    for n in range(parts):
        piece(n).start()
    more[...] = jnp.zeros_like(more)
    for load in loads:
        load.wait()

    def add(n, carry):
        for c, sums in enumerate((total, more)):
            label = labels_ref[n, c, me]
            at = jnp.where(label < 0, blocks, label)
            sums[at] = sums[at] + arrived[n, c].astype(jnp.float32).reshape(total.shape[1:])
        return carry

    for n in range(parts):
        piece(n).wait()
        lax.fori_loop(n * share, (n + 1) * share, add, 0)
    outs = [
        pltpu.make_async_copy(total.at[s], out_hbm.at[:, :, s, :], out_sem.at[s]) for s in range(rows)
    ]
    for s, out in enumerate(outs):
        total[s] = total[s] + more[s]
        if s:
            outs[s - 1].start()
    outs[rows - 1].start()
    for out in outs:
        out.wait()


def body(
    tracers, winds, depart_first, depart_second, fluxes, remap_weights, target_device, target_block
):
    wide = HMAX + 1
    narrow = max((HMAX + 1) // 2 + 1, HMAX // 2 + 2)
    chans, levels, rows, lanes = tracers.shape
    comps = winds.shape[0]
    tiles, links = target_device.shape
    depth, cells = fluxes.shape[1:]
    cols = remap_weights.shape[3]
    blocks = rows * lanes // cols
    devices = lax.axis_size("lat") * lax.axis_size("lon")
    padded = -(-devices // LANES) * LANES
    halves = rows // 8
    dims = (chans, levels, rows, comps, tiles, links, blocks, wide, narrow)
    hbm = pl.BlockSpec(memory_space=pl.ANY)
    vmem = pl.BlockSpec(memory_space=pltpu.VMEM)
    smem = pl.BlockSpec(memory_space=pltpu.SMEM)
    f32, b16, i32 = jnp.float32, jnp.bfloat16, jnp.int32
    dma = pltpu.SemaphoreType.DMA
    moved, arrived, labels = pl.pallas_call(
        functools.partial(step_kernel, dims),
        out_shape=(
            jax.ShapeDtypeStruct((rows, levels, chans, lanes), f32),
            jax.ShapeDtypeStruct((devices, CAP, depth, cols), b16),
            jax.ShapeDtypeStruct((devices, CAP, padded), i32),
        ),
        in_specs=[hbm] * 6 + [smem] * 2,
        out_specs=(hbm, hbm, hbm),
        scratch_shapes=[
            pltpu.VMEM((comps, rows + 2 * wide, levels, lanes), f32),
            pltpu.VMEM((comps, rows, levels, lanes), i32),
            pltpu.VMEM((comps, rows, levels, lanes), i32),
            pltpu.VMEM((levels, rows + 2 * narrow, chans, lanes), f32),
            pltpu.VMEM((tiles, depth, cells), b16),
            pltpu.VMEM((tiles, links, cells, cols), b16),
            pltpu.VMEM((tiles * links, depth, cols), b16),
            pltpu.VMEM((devices, CAP, depth, cols), b16),
            pltpu.VMEM((CAP, padded), i32),
            pltpu.SMEM((CAP, padded), i32),
            pltpu.VMEM((CAP, padded), i32),
            pltpu.VMEM((halves, comps, levels, lanes), f32),
            pltpu.VMEM((rows, chans, lanes), f32),
            pltpu.VMEM((2, halves + 2, comps, levels, lanes), f32),
            pltpu.VMEM((2, rows + 2 * narrow, chans, lanes), f32),
            pltpu.VMEM((5 * (2 * wide + 1), comps, rows + 2 * wide, levels, lanes), f32),
            pltpu.VMEM((levels, rows + 2 * narrow, chans, 3 * lanes), b16),
            pltpu.VMEM((4 * lanes, 2 * lanes), b16),
            pltpu.VMEM((4 * lanes, 2 * lanes), b16),
            pltpu.VMEM((lanes // 16 + 1, 16, lanes), b16),
            pltpu.VMEM((2, 5 + 2 * (2 * wide + 1), levels, lanes), f32),
            pltpu.VMEM((2, comps, levels, lanes), f32),
            pltpu.VMEM((5, rows, levels, lanes), f32),
            pltpu.VMEM((2 * narrow + 1, rows, levels, lanes), f32),
            pltpu.VMEM((4, rows, levels, lanes), f32),
            pltpu.VMEM((rows, levels, lanes), i32),
            pltpu.VMEM((rows, levels, chans, lanes), f32),
            dma((levels,)),
            dma((chans,)),
            dma((levels,)),
            dma((levels,)),
            dma((2,)),
            dma(()),
            dma((rows // 2,)),
            dma((16,)),
            dma((16,)),
            dma((devices,)),
            dma((devices,)),
            dma((devices,)),
            dma((devices,)),
        ],
        compiler_params=pltpu.CompilerParams(
            collective_id=0, has_side_effects=True, vmem_limit_bytes=62 * 1024 * 1024
        ),
        name="step",
    )(winds, depart_first, depart_second, tracers, fluxes, remap_weights, target_device.T, target_block.T)
    share = devices // 4 if devices % 4 == 0 else devices
    out = pl.pallas_call(
        functools.partial(join_kernel, (chans, levels, rows, blocks, share)),
        out_shape=jax.ShapeDtypeStruct((chans, levels, rows, lanes), f32),
        in_specs=[hbm, hbm, smem],
        out_specs=hbm,
        scratch_shapes=[
            pltpu.VMEM((blocks + 1, chans, levels, lanes), f32),
            pltpu.VMEM((blocks + 1, chans, levels, lanes), f32),
            pltpu.VMEM((devices, CAP, depth, cols), b16),
            dma((levels,)),
            dma((devices // share,)),
            dma((rows,)),
        ],
        compiler_params=pltpu.CompilerParams(vmem_limit_bytes=62 * 1024 * 1024),
        name="join",
    )(moved, arrived, labels)
    return out


def solution(mesh):
    in_specs = (
        P(None, None, "lat", "lon"),
        P(None, None, "lat", "lon"),
        P(None, None, "lat", "lon"),
        P(None, None, "lat", "lon"),
        P(("lat", "lon"), None, None),
        P(("lat", "lon"), None, None, None),
        P(("lat", "lon"), None),
        P(("lat", "lon"), None),
    )
    out_specs = P(None, None, "lat", "lon")
    return jax.shard_map(body, mesh=mesh, in_specs=in_specs, out_specs=out_specs, check_vma=False)
```

time: 70.5 us -> 68 us (0.965)
  the two profiles are of different devices: /device:TPU:8 before, /device:TPU:11 now
where the time goes in v2:
time: 68 us; the launch traced here: 67.7 us
  Pallas kernels  67.7 us (100%)
    pallas_call x1, Pallas kernels, body(): pl.pallas_call(functools.partial(step_kernel, dims), out_shape=(jax.Shape...  63.2 us
    pallas_call x1, Pallas kernels, body(): pl.pallas_call(functools.partial(join_kernel, (chans, levels, rows, block...  4.5 us

profile of v2, /device:TPU:11, one launch (start us, length us, event | category | flops | bytes accessed | tf_op | source)
XLA Modules:
  0.0 67.7 jit_solution(17073345815677955826)
XLA Ops:
  0.0 63.2 %step.1 = (f32[16,8,16,128]{3,2,1,0:T(8,128)}, bf16[32,2,128,128]{3,2,1,0:T(8,128)(2,1)}, s32[32,2,128]{2,1,0:T(2,128)}) custom-call(f32[3,8,16,128]{3,2,1,0:T(8,128)} %winds_hbm.1, s32[3,8,16,128]{3,2,1,0:T(8,128)} %first_hbm.1, s32[3,8,16,128]{3,2,1,0:T(8,128)} %second_hbm.1, f32[16,8,16,128]{3,2,1,0:T(8,128)} %tracers_hbm.1, ...), custom_call_target="tpu_custom_call" | custom-call | tf_op jit(solution)/shard_map/step/pallas_call | solution.py:619
  63.2 4.5 %join.1 = f32[16,8,16,128]{3,2,1,0:T(8,128)} custom-call(f32[16,8,16,128]{3,2,1,0:T(8,128)} %get-tuple-element.8.moved_hbm, bf16[32,2,128,128]{3,2,1,0:T(8,128)(2,1)} %get-tuple-element.9.arrived_hbm, s32[32,2,128]{2,1,0:T(2,128)} %get-tuple-element.10.labels_ref), custom_call_target="tpu_custom_call" | custom-call | tf_op jit(solution)/shard_map/join/pallas_call | solution.py:676

commit v3 on v2

--- a/solution.py
+++ b/solution.py
@@ -1,4 +1,5 @@
 import functools
+import math
 
 import jax
 import jax.numpy as jnp
@@ -12,6 +13,10 @@
 MESH = pl.DeviceIdType.MESH
 LANES = 128
 BIG = 1 << 20
+DIRECT_PART = 48
+CODES = 32767.0
+ITEM_LOW = 0.049804688 * 0.00019931793
+ITEM_HIGH = 5.0 * 0.019897461
 
 
 def cubic_weights(frac):
@@ -46,18 +51,25 @@
     return spread
 
 
+def code_range(cells, count):
+    low = math.log(0.98 * cells * ITEM_LOW)
+    high = math.log(1.02 * cells * ITEM_HIGH * count)
+    return low, 2.0 * CODES / (high - low)
+
+
 def step_kernel(
     dims,
     winds_hbm, first_hbm, second_hbm, tracers_hbm, fluxes_hbm, weights_hbm, owner_ref, block_ref,
-    moved_ref, arrived_ref, labels_ref,
+    moved_ref, arrived_ref, labels_ref, dense_ref,
     wind_pad, first_v, second_v, tracer_pad, fluxes_v, weights_v,
-    products, outgoing, codes_v, codes_s, marks_v,
+    products, outgoing, codes_v, codes_s, marks_v, relayed, running, dense_v, table_v, table_s,
     wind_pack, tracer_pack, wind_edge, tracer_edge,
     shifted, lhs, rhs_a, rhs_b, masks, wind_w, wind_sum, lev_w, row_w, col_w, col_at, moved_v,
     wind_sem, tracer_sem, first_sem, second_sem, load_sem, code_sem, moved_sem,
     halo_send, halo_recv, item_send, item_recv, mark_send, mark_recv,
+    relay_send, relay_recv, dense_sem, table_sem,
 ):
-    chans, levels, rows, comps, tiles, links, blocks, wide, narrow = dims
+    chans, levels, rows, comps, tiles, links, blocks, wide, narrow, direct = dims
     lanes = LANES
     taps, reach = 2 * wide + 1, 2 * narrow + 1
     lat, lon = lax.axis_index("lat"), lax.axis_index("lon")
@@ -241,62 +253,182 @@
 
     lax.fori_loop(0, tiles // group, multiply, 0)
 
-    def item_copy(p):
+    half_count = lat_count // 2
+    near = half_count * lon_count
+    base = lat // half_count * half_count
+    near_first = base * lon_count
+    far_first = lax.rem(base + half_count, lat_count) * lon_count
+    mine = me - near_first
+    tail = pl.ds(direct, products.shape[1] - direct)
+    head = pl.ds(0, direct)
+
+    def at_device(p):
+        return (p // lon_count, lax.rem(p, lon_count))
+
+    def near_copy(s):
         return pltpu.make_async_remote_copy(
-            src_ref=outgoing.at[p], dst_ref=arrived_ref.at[me],
-            send_sem=item_send.at[p], recv_sem=item_recv.at[me],
-            device_id=(p // lon_count, lax.rem(p, lon_count)), device_id_type=MESH,
+            src_ref=outgoing.at[near_first + s], dst_ref=arrived_ref.at[me],
+            send_sem=item_send.at[near_first + s], recv_sem=item_recv.at[me],
+            device_id=at_device(near_first + s), device_id_type=MESH,
+        )
+
+    def far_copy(s):
+        return pltpu.make_async_remote_copy(
+            src_ref=outgoing.at[far_first + s, :, head], dst_ref=arrived_ref.at[me, :, head],
+            send_sem=item_send.at[far_first + s], recv_sem=item_recv.at[me],
+            device_id=at_device(far_first + s), device_id_type=MESH,
+        )
+
+    def relay_copy(s):
+        return pltpu.make_async_remote_copy(
+            src_ref=outgoing.at[far_first + s, :, tail], dst_ref=relayed.at[mine],
+            send_sem=relay_send.at[s], recv_sem=relay_recv.at[mine],
+            device_id=at_device(near_first + s), device_id_type=MESH,
         )
 
     def mark_copy(p):
         return pltpu.make_async_remote_copy(
-            src_ref=marks_v, dst_ref=labels_ref.at[me],
+            src_ref=marks_v, dst_ref=labels_ref.at[:, me, :],
             send_sem=mark_send.at[p], recv_sem=mark_recv.at[me],
-            device_id=(p // lon_count, lax.rem(p, lon_count)), device_id_type=MESH,
-        )
-
-    middle = lat_count // 2
-    away = sorted(range(lat_count), key=lambda n: abs(n - middle))
-    last = None
-
-    def peer(there, n):
-        return there * lon_count + lax.rem(lon + n, lon_count)
-
-    for far in away:
-        there = lax.rem(lat + far, lat_count)
-
-        def emit(n, carry, there=there):
-            p = peer(there, n)
+            device_id=at_device(p), device_id_type=MESH,
+        )
+
+    def send_mark(k, carry):
+        mark_copy(lax.rem(me + k, devices)).start()
+        return carry
+
+    lax.fori_loop(1, devices, send_mark, 0)
+
+    def ring(away, n):
+        return lax.rem(lat - base + away, half_count) * lon_count + lax.rem(lon + n, lon_count)
+
+    def fill(first, away):
+        def one(n, carry):
+            p = first + ring(away, n)
             for c in range(CAP):
                 outgoing[p, c] = products[codes_s[c, p]]
-            before = peer(there, n - 1)
-
-            @pl.when(n > 1)
-            def _():
-                item_copy(before).start()
-
-            mark_copy(p).start()
             return carry
 
-        if last is not None:
-            for c in range(CAP):
-                outgoing[peer(there, 0), c] = products[codes_s[c, peer(there, 0)]]
-            item_copy(last).start()
-            if far:
-                item_copy(peer(there, 0)).start()
-                mark_copy(peer(there, 0)).start()
-        else:
-            for c in range(CAP):
-                outgoing[peer(there, 0), c] = products[codes_s[c, peer(there, 0)]]
-            item_copy(peer(there, 0)).start()
-            mark_copy(peer(there, 0)).start()
-        lax.fori_loop(1, lon_count, emit, 0)
-        last = peer(there, lon_count - 1)
-    item_copy(last).start()
-    own_items = pltpu.make_async_copy(outgoing.at[me], arrived_ref.at[me], item_recv.at[me])
-    own_items.start()
-    own_marks = pltpu.make_async_copy(marks_v, labels_ref.at[me], mark_recv.at[me])
-    own_marks.start()
+        lax.fori_loop(0, lon_count, one, 0)
+
+    def send(copy, away, begin):
+        def one(n, carry):
+            copy(ring(away, n)).start()
+            return carry
+
+        lax.fori_loop(begin, lon_count, one, 0)
+
+    for away in list(range(1, half_count)) + [0]:
+        fill(far_first, away)
+        send(relay_copy, away, 0 if away else 1)
+        send(far_copy, away, 0)
+    for away in [0] + list(range(1, half_count)):
+        fill(near_first, away)
+        send(near_copy, away, 0 if away else 1)
+    own_copies = [
+        pltpu.make_async_copy(
+            outgoing.at[far_first + mine, :, tail], relayed.at[mine], relay_recv.at[mine]
+        ),
+        pltpu.make_async_copy(outgoing.at[me], arrived_ref.at[me], item_recv.at[me]),
+        pltpu.make_async_copy(marks_v, labels_ref.at[:, me, :], mark_recv.at[me]),
+    ]
+    for copy in own_copies:
+        copy.start()
+
+    def wait_near(begin, act):
+        def one(k, carry):
+            act(lax.rem(mine + k, near))
+            return carry
+
+        lax.fori_loop(begin, near, one, 0)
+
+    def relay_from(s):
+        return pltpu.make_async_remote_copy(
+            src_ref=outgoing.at[far_first + s, :, tail], dst_ref=relayed.at[s],
+            send_sem=relay_send.at[s], recv_sem=relay_recv.at[s],
+            device_id=at_device(near_first + s), device_id_type=MESH,
+        )
+
+    def mark_from(p):
+        return pltpu.make_async_remote_copy(
+            src_ref=marks_v, dst_ref=labels_ref.at[:, p, :],
+            send_sem=mark_send.at[p], recv_sem=mark_recv.at[p],
+            device_id=at_device(p), device_id_type=MESH,
+        )
+
+    count = CAP * near
+    table_copy = pltpu.make_async_copy(table_v, table_s, table_sem)
+    twin = (far_first + mine) // lon_count
+    dense_copy = pltpu.make_async_remote_copy(
+        src_ref=dense_v, dst_ref=dense_ref, send_sem=dense_sem.at[0], recv_sem=dense_sem.at[1],
+        device_id=(twin, lon), device_id_type=MESH,
+    )
+
+    def sort_relayed():
+        wait_near(1, lambda s: mark_from(near_first + s).wait_recv())
+        own_copies[2].wait()
+        width = table_v.shape[1]
+        sub = lax.broadcasted_iota(jnp.int32, (count, width), 0)
+        lane = lax.broadcasted_iota(jnp.int32, (count, width), 1)
+        spot = lax.broadcasted_iota(jnp.int32, (near, width), 1)
+        column = jnp.concatenate(
+            [
+                jnp.sum(
+                    jnp.where(
+                        spot == far_first + mine,
+                        labels_ref[c, pl.ds(pl.multiple_of(near_first, 8), near), :],
+                        0,
+                    ),
+                    axis=1,
+                    keepdims=True,
+                )
+                for c in range(CAP)
+            ],
+            axis=0,
+        )
+        label = jnp.broadcast_to(jnp.where(column < 0, blocks, column), (count, width))
+        across = jnp.sum(jnp.where(sub == lane, label, 0), axis=0, keepdims=True)
+        across = jnp.broadcast_to(across, (count, width))
+        inside = lane < count
+        before = jnp.logical_or(label < across, jnp.logical_and(label == across, sub < lane))
+        rank = jnp.sum(jnp.where(before, 1, 0), axis=0, keepdims=True)
+        pick = jnp.logical_and(jnp.broadcast_to(rank, (count, width)) == sub, inside)
+        code = lax.rem(lane, near) * CAP + lane // near
+        item = jnp.sum(jnp.where(pick, code, 0), axis=1, keepdims=True)
+        ordered = jnp.sum(jnp.where(pick, across, 0), axis=1, keepdims=True)
+        ordered = jnp.broadcast_to(ordered, (count, width))
+        same = jnp.logical_and(ordered == pltpu.roll(ordered, 1, 0), sub > 0)
+        upto = jnp.sum(jnp.where(jnp.logical_and(across <= sub, inside), 1, 0), axis=1, keepdims=True)
+        equal = jnp.sum(jnp.where(jnp.logical_and(across == sub, inside), 1, 0), axis=1, keepdims=True)
+        final = jnp.where(equal > 0, upto - 1, count)
+        table_v[...] = jnp.where(lane == 0, item, jnp.where(lane == 1, jnp.where(same, 1, 0), final))
+        table_copy.start()
+
+    def sum_relayed():
+        wait_near(1, lambda s: relay_from(s).wait_recv())
+        own_copies[0].wait()
+        table_copy.wait()
+        size = products.shape[1] - direct
+
+        def add(n, total):
+            item = table_s[n, 0]
+            kept = table_s[n, 1].astype(jnp.float32)
+            total = total * kept + relayed[item // CAP, lax.rem(item, CAP)].astype(jnp.float32)
+            running[n] = total
+            return total
+
+        lax.fori_loop(0, count, add, jnp.zeros((size, lanes), jnp.float32))
+        running[count] = jnp.zeros((size, lanes), jnp.float32)
+        low, scale = code_range(fluxes_v.shape[2], count)
+
+        def encode(s, carry):
+            value = running[table_s[s, 2]]
+            code = jnp.round((jnp.log(value) - low) * scale) - CODES
+            code = jnp.where(value > 0.0, jnp.clip(code, -CODES, CODES), -CODES - 1.0)
+            dense_v[s] = code.astype(jnp.int32).astype(jnp.int16)
+            return carry
+
+        lax.fori_loop(0, blocks, encode, 0)
 
     deep, across16 = (
         lax.broadcasted_iota(jnp.int32, (16, lanes), 0),
@@ -304,8 +436,8 @@
     )
     groups = lanes // 16
     for t in range(groups):
-        near = jnp.abs(16 * t + deep - across16) <= narrow
-        masks[t] = jnp.where(near, 1.0, 0.0).astype(jnp.bfloat16)
+        reached = jnp.abs(16 * t + deep - across16) <= narrow
+        masks[t] = jnp.where(reached, 1.0, 0.0).astype(jnp.bfloat16)
     outer = jnp.where(deep < 8, deep - 8, deep + (lanes - 8))
     masks[groups] = jnp.where(jnp.abs(outer - across16) <= narrow, 1.0, 0.0).astype(jnp.bfloat16)
     rhs_a[...] = jnp.zeros_like(rhs_a)
@@ -515,6 +647,9 @@
                 build(0, after, both[0])
             apply(level, pair, both[level % 2])
 
+        pl.when(pair == 1)(sort_relayed)
+        pl.when(pair == 2)(sum_relayed)
+        pl.when(pair == 3)(dense_copy.start)
         for level in range(levels):
             pl.when(pair >= 0)(functools.partial(level_step, level))
         moved_copy(pair).start()
@@ -528,66 +663,97 @@
         copy.wait_send()
     each(has_north, wind_north + tracer_north, leave)
     each(has_south, wind_south + tracer_south, leave)
-    own_items.wait()
-    own_marks.wait()
-
-    def finish(n, carry):
-        p = lax.rem(me + n, devices)
-        where = (p // lon_count, lax.rem(p, lon_count))
-        item_copy(p).wait_send()
-        mark_copy(p).wait_send()
+    own_copies[1].wait()
+
+    def near_done(s):
+        near_copy(s).wait_send()
+        relay_copy(s).wait_send()
+        mark_copy(near_first + s).wait_send()
         pltpu.make_async_remote_copy(
-            src_ref=outgoing.at[p], dst_ref=arrived_ref.at[p],
-            send_sem=item_send.at[p], recv_sem=item_recv.at[p],
-            device_id=where, device_id_type=MESH,
+            src_ref=outgoing.at[near_first + s], dst_ref=arrived_ref.at[near_first + s],
+            send_sem=item_send.at[near_first + s], recv_sem=item_recv.at[near_first + s],
+            device_id=at_device(near_first + s), device_id_type=MESH,
         ).wait_recv()
+
+    def far_done(s):
+        far_copy(s).wait_send()
+        mark_copy(far_first + s).wait_send()
+        mark_from(far_first + s).wait_recv()
         pltpu.make_async_remote_copy(
-            src_ref=marks_v, dst_ref=labels_ref.at[p],
-            send_sem=mark_send.at[p], recv_sem=mark_recv.at[p],
-            device_id=where, device_id_type=MESH,
+            src_ref=outgoing.at[far_first + s, :, head], dst_ref=arrived_ref.at[far_first + s, :, head],
+            send_sem=item_send.at[far_first + s], recv_sem=item_recv.at[far_first + s],
+            device_id=at_device(far_first + s), device_id_type=MESH,
         ).wait_recv()
-        return carry
-
-    lax.fori_loop(1, devices, finish, 0)
-
-
-def join_kernel(dims, moved_hbm, arrived_hbm, labels_ref, out_hbm, total, more, arrived, moved_sem, item_sem, out_sem):
-    chans, levels, rows, blocks, share = dims
-    me = lax.axis_index("lat") * lax.axis_size("lon") + lax.axis_index("lon")
+
+    wait_near(1, near_done)
+    wait_near(0, far_done)
+    dense_copy.wait()
+
+
+def join_kernel(
+    dims, moved_hbm, arrived_hbm, labels_ref, dense_hbm, out_hbm,
+    total, more, near_v, far_v, dense_v, moved_sem, near_sem, far_sem, dense_sem, out_sem,
+):
+    chans, levels, rows, blocks, direct, cells = dims
+    lat_count, lon_count = lax.axis_size("lat"), lax.axis_size("lon")
+    me = lax.axis_index("lat") * lon_count + lax.axis_index("lon")
+    near = near_v.shape[0]
+    near_first = me // near * near
+    far_first = lax.rem(near_first + near, lat_count * lon_count)
+    lanes = total.shape[3]
     loads = [
         pltpu.make_async_copy(
             moved_hbm.at[:, level], total.at[pl.ds(0, rows), :, level, :], moved_sem.at[level]
         )
         for level in range(levels)
     ]
-    for load in loads:
+    near_load = pltpu.make_async_copy(arrived_hbm.at[pl.ds(near_first, near)], near_v, near_sem)
+    far_load = pltpu.make_async_copy(
+        arrived_hbm.at[pl.ds(far_first, near), :, pl.ds(0, direct)], far_v, far_sem
+    )
+    dense_load = pltpu.make_async_copy(dense_hbm, dense_v, dense_sem)
+    for load in loads + [dense_load, near_load, far_load]:
         load.start()
-    parts = arrived.shape[0] // share
-
-    def piece(n):
-        cut = pl.ds(n * share, share)
-        return pltpu.make_async_copy(arrived_hbm.at[cut], arrived.at[cut], item_sem.at[n])
-
-    for n in range(parts):
-        piece(n).start()
     more[...] = jnp.zeros_like(more)
     for load in loads:
         load.wait()
-
-    def add(n, carry):
+    dense_load.wait()
+    low, scale = code_range(cells, CAP * near)
+    cut = direct // levels
+
+    def decode(s, carry):
+        code = dense_v[s].astype(jnp.int32).astype(jnp.float32)
+        value = jnp.exp((code + CODES) * (1.0 / scale) + low)
+        value = jnp.where(code < -CODES, 0.0, value)
+        more[s, cut:] = value.reshape(chans - cut, levels, lanes)
+        return carry
+
+    lax.fori_loop(0, blocks, decode, 0)
+
+    def place(n, c):
+        label = labels_ref[c, n, me]
+        return jnp.where(label < 0, blocks, label)
+
+    def add_near(n, carry):
         for c, sums in enumerate((total, more)):
-            label = labels_ref[n, c, me]
-            at = jnp.where(label < 0, blocks, label)
-            sums[at] = sums[at] + arrived[n, c].astype(jnp.float32).reshape(total.shape[1:])
-        return carry
-
-    for n in range(parts):
-        piece(n).wait()
-        lax.fori_loop(n * share, (n + 1) * share, add, 0)
+            at = place(near_first + n, c)
+            sums[at] = sums[at] + near_v[n, c].astype(jnp.float32).reshape(chans, levels, lanes)
+        return carry
+
+    def add_far(n, carry):
+        for c, sums in enumerate((total, more)):
+            at = place(far_first + n, c)
+            sums[at, :cut] = sums[at, :cut] + far_v[n, c].astype(jnp.float32).reshape(cut, levels, lanes)
+        return carry
+
+    near_load.wait()
+    lax.fori_loop(0, near, add_near, 0)
+    far_load.wait()
+    lax.fori_loop(0, near, add_far, 0)
     outs = [
         pltpu.make_async_copy(total.at[s], out_hbm.at[:, :, s, :], out_sem.at[s]) for s in range(rows)
     ]
-    for s, out in enumerate(outs):
+    for s in range(rows):
         total[s] = total[s] + more[s]
         if s:
             outs[s - 1].start()
@@ -610,21 +776,24 @@
     devices = lax.axis_size("lat") * lax.axis_size("lon")
     padded = -(-devices // LANES) * LANES
     halves = rows // 8
-    dims = (chans, levels, rows, comps, tiles, links, blocks, wide, narrow)
+    direct = depth * DIRECT_PART // 128 // 16 * 16
+    near = devices // 2
+    dims = (chans, levels, rows, comps, tiles, links, blocks, wide, narrow, direct)
     hbm = pl.BlockSpec(memory_space=pl.ANY)
     vmem = pl.BlockSpec(memory_space=pltpu.VMEM)
     smem = pl.BlockSpec(memory_space=pltpu.SMEM)
     f32, b16, i32 = jnp.float32, jnp.bfloat16, jnp.int32
     dma = pltpu.SemaphoreType.DMA
-    moved, arrived, labels = pl.pallas_call(
+    moved, arrived, labels, dense = pl.pallas_call(
         functools.partial(step_kernel, dims),
         out_shape=(
             jax.ShapeDtypeStruct((rows, levels, chans, lanes), f32),
             jax.ShapeDtypeStruct((devices, CAP, depth, cols), b16),
-            jax.ShapeDtypeStruct((devices, CAP, padded), i32),
+            jax.ShapeDtypeStruct((CAP, devices, padded), i32),
+            jax.ShapeDtypeStruct((blocks, depth - direct, cols), jnp.int16),
         ),
         in_specs=[hbm] * 6 + [smem] * 2,
-        out_specs=(hbm, hbm, hbm),
+        out_specs=(hbm, hbm, vmem, hbm),
         scratch_shapes=[
             pltpu.VMEM((comps, rows + 2 * wide, levels, lanes), f32),
             pltpu.VMEM((comps, rows, levels, lanes), i32),
@@ -637,6 +806,11 @@
             pltpu.VMEM((CAP, padded), i32),
             pltpu.SMEM((CAP, padded), i32),
             pltpu.VMEM((CAP, padded), i32),
+            pltpu.VMEM((near, CAP, depth - direct, cols), b16),
+            pltpu.VMEM((near * CAP + 1, depth - direct, cols), f32),
+            pltpu.VMEM((blocks, depth - direct, cols), jnp.int16),
+            pltpu.VMEM((near * CAP, padded), i32),
+            pltpu.SMEM((near * CAP, padded), i32),
             pltpu.VMEM((halves, comps, levels, lanes), f32),
             pltpu.VMEM((rows, chans, lanes), f32),
             pltpu.VMEM((2, halves + 2, comps, levels, lanes), f32),
@@ -666,30 +840,36 @@
             dma((devices,)),
             dma((devices,)),
             dma((devices,)),
+            dma((near,)),
+            dma((near,)),
+            dma((2,)),
+            dma(()),
         ],
         compiler_params=pltpu.CompilerParams(
             collective_id=0, has_side_effects=True, vmem_limit_bytes=62 * 1024 * 1024
         ),
         name="step",
     )(winds, depart_first, depart_second, tracers, fluxes, remap_weights, target_device.T, target_block.T)
-    share = devices // 4 if devices % 4 == 0 else devices
-    out = pl.pallas_call(
-        functools.partial(join_kernel, (chans, levels, rows, blocks, share)),
+    return pl.pallas_call(
+        functools.partial(join_kernel, (chans, levels, rows, blocks, direct, cells)),
         out_shape=jax.ShapeDtypeStruct((chans, levels, rows, lanes), f32),
-        in_specs=[hbm, hbm, smem],
+        in_specs=[hbm, hbm, smem, hbm],
         out_specs=hbm,
         scratch_shapes=[
             pltpu.VMEM((blocks + 1, chans, levels, lanes), f32),
             pltpu.VMEM((blocks + 1, chans, levels, lanes), f32),
-            pltpu.VMEM((devices, CAP, depth, cols), b16),
+            pltpu.VMEM((near, CAP, depth, cols), b16),
+            pltpu.VMEM((near, CAP, direct, cols), b16),
+            pltpu.VMEM((blocks, depth - direct, cols), jnp.int16),
             dma((levels,)),
-            dma((devices // share,)),
+            dma(()),
+            dma(()),
+            dma(()),
             dma((rows,)),
         ],
         compiler_params=pltpu.CompilerParams(vmem_limit_bytes=62 * 1024 * 1024),
         name="join",
-    )(moved, arrived, labels)
-    return out
+    )(moved, arrived, labels, dense)
 
 
 def solution(mesh):

time: 68 us -> 58.2 us (0.86)
  the two profiles are of different devices: /device:TPU:11 before, /device:TPU:0 now
where the time goes in v3:
time: 58.2 us; the launch traced here: 58 us
  Pallas kernels  58 us (100%)
    pallas_call x1, Pallas kernels, body(): pl.pallas_call(functools.partial(step_kernel, dims), out_shape=(jax.Shape...  53.3 us
    pallas_call x1, Pallas kernels, body(): pl.pallas_call(functools.partial(join_kernel, (chans, levels, rows, block...  4.66 us

profile of v3, /device:TPU:0, one launch (start us, length us, event | category | flops | bytes accessed | tf_op | source)
XLA Modules:
  0.0 58.0 jit_solution(17560707617995201270)
XLA Ops:
  0.0 53.3 %step.1 = (f32[16,8,16,128]{3,2,1,0:T(8,128)}, bf16[32,2,128,128]{3,2,1,0:T(8,128)(2,1)}, s32[2,32,128]{2,1,0:T(8,128)}, s16[16,80,128]{2,1,0:T(8,128)(2,1)}) custom-call(f32[3,8,16,128]{3,2,1,0:T(8,128)} %winds_hbm.1, s32[3,8,16,128]{3,2,1,0:T(8,128)} %first_hbm.1, s32[3,8,16,128]{3,2,1,0:T(8,128)} %second_hbm.1, f32[16,8,16,128]{3,2,1,0:T(8,128)} %tracers_hbm.1, ...), custom_call_target="tpu_custom_call" | custom-call | tf_op jit(solution)/shard_map/step/pallas_call | solution.py:787
  53.3 4.7 %join.1 = f32[16,8,16,128]{3,2,1,0:T(8,128)} custom-call(f32[16,8,16,128]{3,2,1,0:T(8,128)} %get-tuple-element.9.moved_hbm, bf16[32,2,128,128]{3,2,1,0:T(8,128)(2,1)} %get-tuple-element.10.arrived_hbm, s32[2,32,128]{2,1,0:T(8,128)} %get-tuple-element.11.labels_ref, s16[16,80,128]{2,1,0:T(8,128)(2,1)} %get-tuple-element.12.dense_hbm), custom_call_target="tpu_custom_call" | custom-call | tf_op jit(solution)/shard_map/join/pallas_call | solution.py:853

commit v4 on v3

--- a/solution.py
+++ b/solution.py
@@ -59,15 +59,15 @@
 
 def step_kernel(
     dims,
-    winds_hbm, first_hbm, second_hbm, tracers_hbm, fluxes_hbm, weights_hbm, owner_ref, block_ref,
-    moved_ref, arrived_ref, labels_ref, dense_ref,
+    winds_hbm, first_hbm, second_hbm, tracers_hbm, fluxes_hbm, weights_hbm, owner_hbm, block_hbm,
+    moved_ref, arrived_ref, labels_out, dense_ref,
+    owner_ref, block_ref, labels_ref,
     wind_pad, first_v, second_v, tracer_pad, fluxes_v, weights_v,
     products, outgoing, codes_v, codes_s, marks_v, relayed, running, dense_v, table_v, table_s,
     wind_pack, tracer_pack, wind_edge, tracer_edge,
     shifted, lhs, rhs_a, rhs_b, masks, wind_w, wind_sum, lev_w, row_w, col_w, col_at, moved_v,
-    wind_sem, tracer_sem, first_sem, second_sem, load_sem, code_sem, moved_sem,
-    halo_send, halo_recv, item_send, item_recv, mark_send, mark_recv,
-    relay_send, relay_recv, dense_sem, table_sem,
+    load_sem, code_sem, moved_sem, halo_send, halo_recv, near_sem, far_sem, mark_sem, relay_sem,
+    dense_sem, table_sem, own_sem, labels_sem,
 ):
     chans, levels, rows, comps, tiles, links, blocks, wide, narrow, direct = dims
     lanes = LANES
@@ -77,37 +77,140 @@
     devices = lat_count * lon_count
     me = lat * lon_count + lon
 
-    def by_level(source, target, sem, start):
+    def by_level(source, target, n, start):
         return [
             pltpu.make_async_copy(
-                source.at[:, level], target.at[:, pl.ds(start, rows), level, :], sem.at[level]
+                source.at[:, level], target.at[:, pl.ds(start, rows), level, :], load_sem.at[n]
             )
             for level in range(levels)
         ]
 
-    wind_loads = by_level(winds_hbm, wind_pad, wind_sem, wide)
+    def whole(ref, sem):
+        return pltpu.make_async_copy(ref, ref, sem)
+
+    tables = [
+        pltpu.make_async_copy(owner_hbm, owner_ref, load_sem.at[6]),
+        pltpu.make_async_copy(block_hbm, block_ref, load_sem.at[7]),
+    ]
+    wind_loads = by_level(winds_hbm, wind_pad, 2, wide)
     tracer_loads = [
         pltpu.make_async_copy(
-            tracers_hbm.at[chan], tracer_pad.at[:, pl.ds(narrow, rows), chan, :], tracer_sem.at[chan]
+            tracers_hbm.at[chan], tracer_pad.at[:, pl.ds(narrow, rows), chan, :], load_sem.at[3]
         )
         for chan in range(chans)
     ]
     flux_load = pltpu.make_async_copy(fluxes_hbm, fluxes_v, load_sem.at[0])
     weight_load = pltpu.make_async_copy(weights_hbm, weights_v, load_sem.at[1])
-    late_loads = by_level(first_hbm, first_v, first_sem, 0) + by_level(second_hbm, second_v, second_sem, 0)
-    for load in wind_loads + tracer_loads + [flux_load, weight_load] + late_loads:
+    late_loads = by_level(first_hbm, first_v, 4, 0) + by_level(second_hbm, second_v, 5, 0)
+    for load in wind_loads + tracer_loads + tables + [flux_load, weight_load] + late_loads:
         load.start()
+    inner_winds = wind_pad.at[:, pl.ds(wide, rows)]
+    inner_tracers = tracer_pad.at[:, pl.ds(narrow, rows)]
 
     barrier = pltpu.get_barrier_semaphore()
 
-    def greet(k, carry):
-        p = lax.rem(me + k, devices)
-        pl.semaphore_signal(
-            barrier, inc=1, device_id=(p // lon_count, lax.rem(p, lon_count)), device_id_type=MESH
+    for away in range(lat_count):
+        there = lax.rem(lat + away, lat_count)
+
+        def greet(n, carry, there=there):
+            pl.semaphore_signal(
+                barrier, inc=1, device_id=(there, lax.rem(lon + n, lon_count)), device_id_type=MESH
+            )
+            return carry
+
+        lax.fori_loop(0 if away else 1, lon_count, greet, 0)
+
+    lane8 = lax.broadcasted_iota(jnp.int32, (levels, lanes), 1)
+    lane16 = lax.broadcasted_iota(jnp.int32, (chans, lanes), 1)
+    west, east = lax.rem(lon + lon_count - 1, lon_count), lax.rem(lon + 1, lon_count)
+    north, south = lat - 1, lat + 1
+    has_north, has_south = lat > 0, lat < lat_count - 1
+    halves = rows // 8
+
+    def halo(n, source, target, where):
+        return pltpu.make_async_remote_copy(
+            src_ref=source, dst_ref=target, send_sem=halo_send.at[n], recv_sem=halo_recv.at[n],
+            device_id=where, device_id_type=MESH,
         )
+
+    wind_sides = [
+        halo(0, wind_pack, wind_edge.at[0, pl.ds(1, halves)], (lat, east)),
+        halo(1, wind_pack, wind_edge.at[1, pl.ds(1, halves)], (lat, west)),
+    ]
+    wind_north = [
+        halo(2, wind_pad.at[:, pl.ds(wide, wide)], wind_pad.at[:, pl.ds(wide + rows, wide)], (north, lon)),
+        halo(3, wind_pack.at[0], wind_edge.at[0, halves + 1], (north, east)),
+        halo(4, wind_pack.at[0], wind_edge.at[1, halves + 1], (north, west)),
+    ]
+    wind_south = [
+        halo(5, wind_pad.at[:, pl.ds(rows, wide)], wind_pad.at[:, pl.ds(0, wide)], (south, lon)),
+        halo(6, wind_pack.at[halves - 1], wind_edge.at[0, 0], (south, east)),
+        halo(7, wind_pack.at[halves - 1], wind_edge.at[1, 0], (south, west)),
+    ]
+    first_rows, last_rows = pl.ds(0, narrow), pl.ds(rows - narrow, narrow)
+    above_rows, below_rows = pl.ds(0, narrow), pl.ds(narrow + rows, narrow)
+    tracer_sides = [
+        halo(8, tracer_pack, tracer_edge.at[0, pl.ds(narrow, rows)], (lat, east)),
+        halo(9, tracer_pack, tracer_edge.at[1, pl.ds(narrow, rows)], (lat, west)),
+    ]
+    tracer_north = [
+        halo(10, tracer_pad.at[:, pl.ds(narrow, narrow)], tracer_pad.at[:, below_rows], (north, lon)),
+        halo(11, tracer_pack.at[first_rows], tracer_edge.at[0, below_rows], (north, east)),
+        halo(12, tracer_pack.at[first_rows], tracer_edge.at[1, below_rows], (north, west)),
+    ]
+    tracer_south = [
+        halo(13, tracer_pad.at[:, pl.ds(rows, narrow)], tracer_pad.at[:, above_rows], (south, lon)),
+        halo(14, tracer_pack.at[last_rows], tracer_edge.at[0, above_rows], (south, east)),
+        halo(15, tracer_pack.at[last_rows], tracer_edge.at[1, above_rows], (south, west)),
+    ]
+
+    def each(condition, copies, act):
+        @pl.when(condition)
+        def _():
+            for copy in copies:
+                act(copy)
+
+    start, arrive, leave = (lambda c: c.start()), (lambda c: c.wait_recv()), (lambda c: c.wait_send())
+    whole(inner_winds, load_sem.at[2]).wait()
+    whole(inner_tracers, load_sem.at[3]).wait()
+    pl.semaphore_wait(barrier, devices - 1)
+    each(has_north, [wind_north[0], tracer_north[0]], start)
+    each(has_south, [wind_south[0], tracer_south[0]], start)
+
+    for half in range(halves):
+        for comp in range(comps):
+            packed = jnp.zeros((levels, lanes), jnp.float32)
+            for p in range(8):
+                value = wind_pad[comp, wide + half * 8 + p]
+                packed = jnp.where(
+                    lane8 // 16 == p, pltpu.roll(value, (16 * p + 8) % lanes, 1), packed
+                )
+            wind_pack[half, comp] = packed
+
+    each(has_north, wind_north[1:], start)
+    each(has_south, wind_south[1:], start)
+    for copy in wind_sides:
+        copy.start()
+
+    def pack_row(r, carry):
+        for side in range(2):
+            packed = jnp.zeros((chans, lanes), jnp.float32)
+            for level in range(levels):
+                value = tracer_pad[level, narrow + 2 * r + side]
+                packed = jnp.where(
+                    lane16 // 16 == level, pltpu.roll(value, (16 * level + 8) % lanes, 1), packed
+                )
+            tracer_pack[2 * r + side] = packed
         return carry
 
-    lax.fori_loop(1, devices, greet, 0)
+    lax.fori_loop(0, rows // 2, pack_row, 0)
+
+    each(has_north, tracer_north[1:], start)
+    each(has_south, tracer_south[1:], start)
+    for copy in tracer_sides:
+        copy.start()
+    for load in tables:
+        load.wait()
 
     width = codes_v.shape[1]
     spot = lax.broadcasted_iota(jnp.int32, (1, width), 1)
@@ -134,40 +237,6 @@
     code_copy = pltpu.make_async_copy(codes_v, codes_s, code_sem)
     code_copy.start()
 
-    lane8 = lax.broadcasted_iota(jnp.int32, (levels, lanes), 1)
-    lane16 = lax.broadcasted_iota(jnp.int32, (chans, lanes), 1)
-    west, east = lax.rem(lon + lon_count - 1, lon_count), lax.rem(lon + 1, lon_count)
-    north, south = lat - 1, lat + 1
-    has_north, has_south = lat > 0, lat < lat_count - 1
-    halves = rows // 8
-
-    for load in wind_loads:
-        load.wait()
-    for half in range(halves):
-        for comp in range(comps):
-            packed = jnp.zeros((levels, lanes), jnp.float32)
-            for p in range(8):
-                value = wind_pad[comp, wide + half * 8 + p]
-                packed = jnp.where(
-                    lane8 // 16 == p, pltpu.roll(value, (16 * p + 8) % lanes, 1), packed
-                )
-            wind_pack[half, comp] = packed
-    for load in tracer_loads:
-        load.wait()
-
-    def pack_row(r, carry):
-        for side in range(2):
-            packed = jnp.zeros((chans, lanes), jnp.float32)
-            for level in range(levels):
-                value = tracer_pad[level, narrow + 2 * r + side]
-                packed = jnp.where(
-                    lane16 // 16 == level, pltpu.roll(value, (16 * level + 8) % lanes, 1), packed
-                )
-            tracer_pack[2 * r + side] = packed
-        return carry
-
-    lax.fori_loop(0, rows // 2, pack_row, 0)
-
     @pl.when(jnp.logical_not(has_north))
     def _():
         wind_pad[:, 0:wide] = jnp.zeros((comps, wide, levels, lanes), jnp.float32)
@@ -181,61 +250,6 @@
         wind_edge[:, halves + 1] = jnp.zeros((2, comps, levels, lanes), jnp.float32)
         tracer_pad[:, narrow + rows :] = jnp.zeros((levels, narrow, chans, lanes), jnp.float32)
         tracer_edge[:, narrow + rows :] = jnp.zeros((2, narrow, chans, lanes), jnp.float32)
-
-    pl.semaphore_wait(barrier, devices - 1)
-
-    def halo(n, source, target, where):
-        return pltpu.make_async_remote_copy(
-            src_ref=source, dst_ref=target, send_sem=halo_send.at[n], recv_sem=halo_recv.at[n],
-            device_id=where, device_id_type=MESH,
-        )
-
-    wind_sides = [
-        halo(0, wind_pack, wind_edge.at[0, pl.ds(1, halves)], (lat, east)),
-        halo(1, wind_pack, wind_edge.at[1, pl.ds(1, halves)], (lat, west)),
-    ]
-    wind_north = [
-        halo(2, wind_pad.at[:, pl.ds(wide, wide)], wind_pad.at[:, pl.ds(wide + rows, wide)], (north, lon)),
-        halo(3, wind_pack.at[0], wind_edge.at[0, halves + 1], (north, east)),
-        halo(4, wind_pack.at[0], wind_edge.at[1, halves + 1], (north, west)),
-    ]
-    wind_south = [
-        halo(5, wind_pad.at[:, pl.ds(rows, wide)], wind_pad.at[:, pl.ds(0, wide)], (south, lon)),
-        halo(6, wind_pack.at[halves - 1], wind_edge.at[0, 0], (south, east)),
-        halo(7, wind_pack.at[halves - 1], wind_edge.at[1, 0], (south, west)),
-    ]
-    first_rows, last_rows = pl.ds(0, narrow), pl.ds(rows - narrow, narrow)
-    above_rows, below_rows = pl.ds(0, narrow), pl.ds(narrow + rows, narrow)
-    tracer_sides = [
-        halo(8, tracer_pack, tracer_edge.at[0, pl.ds(narrow, rows)], (lat, east)),
-        halo(9, tracer_pack, tracer_edge.at[1, pl.ds(narrow, rows)], (lat, west)),
-    ]
-    tracer_north = [
-        halo(10, tracer_pad.at[:, pl.ds(narrow, narrow)], tracer_pad.at[:, below_rows], (north, lon)),
-        halo(11, tracer_pack.at[first_rows], tracer_edge.at[0, below_rows], (north, east)),
-        halo(12, tracer_pack.at[first_rows], tracer_edge.at[1, below_rows], (north, west)),
-    ]
-    tracer_south = [
-        halo(13, tracer_pad.at[:, pl.ds(rows, narrow)], tracer_pad.at[:, above_rows], (south, lon)),
-        halo(14, tracer_pack.at[last_rows], tracer_edge.at[0, above_rows], (south, east)),
-        halo(15, tracer_pack.at[last_rows], tracer_edge.at[1, above_rows], (south, west)),
-    ]
-
-    def each(condition, copies, act):
-        @pl.when(condition)
-        def _():
-            for copy in copies:
-                act(copy)
-
-    start, arrive, leave = (lambda c: c.start()), (lambda c: c.wait_recv()), (lambda c: c.wait_send())
-    each(has_north, wind_north, start)
-    each(has_south, wind_south, start)
-    for copy in wind_sides:
-        copy.start()
-    each(has_north, tracer_north, start)
-    each(has_south, tracer_south, start)
-    for copy in tracer_sides:
-        copy.start()
 
     code_copy.wait()
     flux_load.wait()
@@ -268,36 +282,38 @@
     def near_copy(s):
         return pltpu.make_async_remote_copy(
             src_ref=outgoing.at[near_first + s], dst_ref=arrived_ref.at[me],
-            send_sem=item_send.at[near_first + s], recv_sem=item_recv.at[me],
+            send_sem=near_sem.at[0], recv_sem=near_sem.at[1],
             device_id=at_device(near_first + s), device_id_type=MESH,
         )
 
     def far_copy(s):
         return pltpu.make_async_remote_copy(
             src_ref=outgoing.at[far_first + s, :, head], dst_ref=arrived_ref.at[me, :, head],
-            send_sem=item_send.at[far_first + s], recv_sem=item_recv.at[me],
+            send_sem=far_sem.at[0], recv_sem=far_sem.at[1],
             device_id=at_device(far_first + s), device_id_type=MESH,
         )
 
     def relay_copy(s):
         return pltpu.make_async_remote_copy(
             src_ref=outgoing.at[far_first + s, :, tail], dst_ref=relayed.at[mine],
-            send_sem=relay_send.at[s], recv_sem=relay_recv.at[mine],
+            send_sem=relay_sem.at[0], recv_sem=relay_sem.at[1],
             device_id=at_device(near_first + s), device_id_type=MESH,
         )
 
-    def mark_copy(p):
-        return pltpu.make_async_remote_copy(
-            src_ref=marks_v, dst_ref=labels_ref.at[:, me, :],
-            send_sem=mark_send.at[p], recv_sem=mark_recv.at[me],
-            device_id=at_device(p), device_id_type=MESH,
-        )
-
-    def send_mark(k, carry):
-        mark_copy(lax.rem(me + k, devices)).start()
-        return carry
-
-    lax.fori_loop(1, devices, send_mark, 0)
+    def send_marks(first, recv, begin):
+        def one(k, carry):
+            s = lax.rem(mine + k, near)
+            pltpu.make_async_remote_copy(
+                src_ref=marks_v, dst_ref=labels_ref.at[:, me, :],
+                send_sem=mark_sem.at[0], recv_sem=mark_sem.at[recv],
+                device_id=at_device(first + s), device_id_type=MESH,
+            ).start()
+            return carry
+
+        lax.fori_loop(begin, near, one, 0)
+
+    send_marks(near_first, 1, 1)
+    send_marks(far_first, 2, 0)
 
     def ring(away, n):
         return lax.rem(lat - base + away, half_count) * lon_count + lax.rem(lon + n, lon_count)
@@ -327,34 +343,16 @@
         send(near_copy, away, 0 if away else 1)
     own_copies = [
         pltpu.make_async_copy(
-            outgoing.at[far_first + mine, :, tail], relayed.at[mine], relay_recv.at[mine]
+            outgoing.at[far_first + mine, :, tail], relayed.at[mine], own_sem.at[0]
         ),
-        pltpu.make_async_copy(outgoing.at[me], arrived_ref.at[me], item_recv.at[me]),
-        pltpu.make_async_copy(marks_v, labels_ref.at[:, me, :], mark_recv.at[me]),
+        pltpu.make_async_copy(outgoing.at[me], arrived_ref.at[me], own_sem.at[1]),
+        pltpu.make_async_copy(marks_v, labels_ref.at[:, me, :], own_sem.at[2]),
     ]
     for copy in own_copies:
         copy.start()
 
-    def wait_near(begin, act):
-        def one(k, carry):
-            act(lax.rem(mine + k, near))
-            return carry
-
-        lax.fori_loop(begin, near, one, 0)
-
-    def relay_from(s):
-        return pltpu.make_async_remote_copy(
-            src_ref=outgoing.at[far_first + s, :, tail], dst_ref=relayed.at[s],
-            send_sem=relay_send.at[s], recv_sem=relay_recv.at[s],
-            device_id=at_device(near_first + s), device_id_type=MESH,
-        )
-
-    def mark_from(p):
-        return pltpu.make_async_remote_copy(
-            src_ref=marks_v, dst_ref=labels_ref.at[:, p, :],
-            send_sem=mark_send.at[p], recv_sem=mark_recv.at[p],
-            device_id=at_device(p), device_id_type=MESH,
-        )
+    others = pl.ds(0, near - 1)
+    labels_copy = pltpu.make_async_copy(labels_ref, labels_out, labels_sem)
 
     count = CAP * near
     table_copy = pltpu.make_async_copy(table_v, table_s, table_sem)
@@ -365,7 +363,7 @@
     )
 
     def sort_relayed():
-        wait_near(1, lambda s: mark_from(near_first + s).wait_recv())
+        whole(labels_ref.at[:, others], mark_sem.at[1]).wait()
         own_copies[2].wait()
         width = table_v.shape[1]
         sub = lax.broadcasted_iota(jnp.int32, (count, width), 0)
@@ -404,8 +402,12 @@
         table_v[...] = jnp.where(lane == 0, item, jnp.where(lane == 1, jnp.where(same, 1, 0), final))
         table_copy.start()
 
+    def take_labels():
+        whole(labels_ref.at[:, pl.ds(0, near)], mark_sem.at[2]).wait()
+        labels_copy.start()
+
     def sum_relayed():
-        wait_near(1, lambda s: relay_from(s).wait_recv())
+        whole(relayed.at[others], relay_sem.at[1]).wait()
         own_copies[0].wait()
         table_copy.wait()
         size = products.shape[1] - direct
@@ -443,8 +445,8 @@
     rhs_a[...] = jnp.zeros_like(rhs_a)
     rhs_b[...] = jnp.zeros_like(rhs_b)
 
-    for load in late_loads:
-        load.wait()
+    whole(first_v, load_sem.at[4]).wait()
+    whole(second_v, load_sem.at[5]).wait()
     for copy in wind_sides:
         copy.wait_recv()
     each(has_north, wind_south, arrive)
@@ -626,7 +628,7 @@
 
     def moved_copy(pair):
         return pltpu.make_async_copy(
-            moved_v.at[pl.ds(pair * 2, 2)], moved_ref.at[pl.ds(pair * 2, 2)], moved_sem.at[pair]
+            moved_v.at[pl.ds(pair * 2, 2)], moved_ref.at[pl.ds(pair * 2, 2)], moved_sem
         )
 
     def pair_step(pair, carry):
@@ -650,14 +652,14 @@
         pl.when(pair == 1)(sort_relayed)
         pl.when(pair == 2)(sum_relayed)
         pl.when(pair == 3)(dense_copy.start)
+        pl.when(pair == pairs - 1)(take_labels)
         for level in range(levels):
             pl.when(pair >= 0)(functools.partial(level_step, level))
         moved_copy(pair).start()
         return carry
 
     lax.fori_loop(0, pairs, pair_step, 0)
-    for pair in range(pairs):
-        moved_copy(pair).wait()
+    whole(moved_v, moved_sem).wait()
 
     for copy in wind_sides + tracer_sides:
         copy.wait_send()
@@ -665,34 +667,19 @@
     each(has_south, wind_south + tracer_south, leave)
     own_copies[1].wait()
 
-    def near_done(s):
-        near_copy(s).wait_send()
-        relay_copy(s).wait_send()
-        mark_copy(near_first + s).wait_send()
-        pltpu.make_async_remote_copy(
-            src_ref=outgoing.at[near_first + s], dst_ref=arrived_ref.at[near_first + s],
-            send_sem=item_send.at[near_first + s], recv_sem=item_recv.at[near_first + s],
-            device_id=at_device(near_first + s), device_id_type=MESH,
-        ).wait_recv()
-
-    def far_done(s):
-        far_copy(s).wait_send()
-        mark_copy(far_first + s).wait_send()
-        mark_from(far_first + s).wait_recv()
-        pltpu.make_async_remote_copy(
-            src_ref=outgoing.at[far_first + s, :, head], dst_ref=arrived_ref.at[far_first + s, :, head],
-            send_sem=item_send.at[far_first + s], recv_sem=item_recv.at[far_first + s],
-            device_id=at_device(far_first + s), device_id_type=MESH,
-        ).wait_recv()
-
-    wait_near(1, near_done)
-    wait_near(0, far_done)
+    whole(outgoing.at[others], near_sem.at[0]).wait()
+    whole(outgoing.at[pl.ds(0, near), :, head], far_sem.at[0]).wait()
+    whole(outgoing.at[others, :, tail], relay_sem.at[0]).wait()
+    whole(labels_ref.at[:, pl.ds(0, devices - 1)], mark_sem.at[0]).wait()
+    labels_copy.wait()
+    whole(outgoing.at[pl.ds(0, near), :, head], far_sem.at[1]).wait()
+    whole(outgoing.at[others], near_sem.at[1]).wait()
     dense_copy.wait()
 
 
 def join_kernel(
-    dims, moved_hbm, arrived_hbm, labels_ref, dense_hbm, out_hbm,
-    total, more, near_v, far_v, dense_v, moved_sem, near_sem, far_sem, dense_sem, out_sem,
+    dims, moved_hbm, arrived_hbm, labels_hbm, dense_hbm, out_hbm,
+    labels_ref, total, sums, more, near_v, far_v, dense_v, load_sem, out_sem,
 ):
     chans, levels, rows, blocks, direct, cells = dims
     lat_count, lon_count = lax.axis_size("lat"), lax.axis_size("lon")
@@ -701,22 +688,20 @@
     near_first = me // near * near
     far_first = lax.rem(near_first + near, lat_count * lon_count)
     lanes = total.shape[3]
+    label_load = pltpu.make_async_copy(labels_hbm, labels_ref, load_sem.at[0])
+    near_load = pltpu.make_async_copy(arrived_hbm.at[pl.ds(near_first, near)], near_v, load_sem.at[1])
+    far_load = pltpu.make_async_copy(
+        arrived_hbm.at[pl.ds(far_first, near), :, pl.ds(0, direct)], far_v, load_sem.at[2]
+    )
+    dense_load = pltpu.make_async_copy(dense_hbm, dense_v, load_sem.at[3])
     loads = [
-        pltpu.make_async_copy(
-            moved_hbm.at[:, level], total.at[pl.ds(0, rows), :, level, :], moved_sem.at[level]
-        )
+        pltpu.make_async_copy(moved_hbm.at[:, level], total.at[:, :, level, :], load_sem.at[4])
         for level in range(levels)
     ]
-    near_load = pltpu.make_async_copy(arrived_hbm.at[pl.ds(near_first, near)], near_v, near_sem)
-    far_load = pltpu.make_async_copy(
-        arrived_hbm.at[pl.ds(far_first, near), :, pl.ds(0, direct)], far_v, far_sem
-    )
-    dense_load = pltpu.make_async_copy(dense_hbm, dense_v, dense_sem)
-    for load in loads + [dense_load, near_load, far_load]:
+    for load in [label_load, dense_load, near_load, far_load] + loads:
         load.start()
+    sums[...] = jnp.zeros_like(sums)
     more[...] = jnp.zeros_like(more)
-    for load in loads:
-        load.wait()
     dense_load.wait()
     low, scale = code_range(cells, CAP * near)
     cut = direct // levels
@@ -735,17 +720,18 @@
         return jnp.where(label < 0, blocks, label)
 
     def add_near(n, carry):
-        for c, sums in enumerate((total, more)):
+        for c, one in enumerate((sums, more)):
             at = place(near_first + n, c)
-            sums[at] = sums[at] + near_v[n, c].astype(jnp.float32).reshape(chans, levels, lanes)
+            one[at] = one[at] + near_v[n, c].astype(jnp.float32).reshape(chans, levels, lanes)
         return carry
 
     def add_far(n, carry):
-        for c, sums in enumerate((total, more)):
+        for c, one in enumerate((sums, more)):
             at = place(far_first + n, c)
-            sums[at, :cut] = sums[at, :cut] + far_v[n, c].astype(jnp.float32).reshape(cut, levels, lanes)
+            one[at, :cut] = one[at, :cut] + far_v[n, c].astype(jnp.float32).reshape(cut, levels, lanes)
         return carry
 
+    label_load.wait()
     near_load.wait()
     lax.fori_loop(0, near, add_near, 0)
     far_load.wait()
@@ -753,8 +739,9 @@
     outs = [
         pltpu.make_async_copy(total.at[s], out_hbm.at[:, :, s, :], out_sem.at[s]) for s in range(rows)
     ]
+    pltpu.make_async_copy(total, total, load_sem.at[4]).wait()
     for s in range(rows):
-        total[s] = total[s] + more[s]
+        total[s] = total[s] + (sums[s] + more[s])
         if s:
             outs[s - 1].start()
     outs[rows - 1].start()
@@ -780,8 +767,6 @@
     near = devices // 2
     dims = (chans, levels, rows, comps, tiles, links, blocks, wide, narrow, direct)
     hbm = pl.BlockSpec(memory_space=pl.ANY)
-    vmem = pl.BlockSpec(memory_space=pltpu.VMEM)
-    smem = pl.BlockSpec(memory_space=pltpu.SMEM)
     f32, b16, i32 = jnp.float32, jnp.bfloat16, jnp.int32
     dma = pltpu.SemaphoreType.DMA
     moved, arrived, labels, dense = pl.pallas_call(
@@ -792,9 +777,12 @@
             jax.ShapeDtypeStruct((CAP, devices, padded), i32),
             jax.ShapeDtypeStruct((blocks, depth - direct, cols), jnp.int16),
         ),
-        in_specs=[hbm] * 6 + [smem] * 2,
-        out_specs=(hbm, hbm, vmem, hbm),
+        in_specs=[hbm] * 8,
+        out_specs=(hbm, hbm, hbm, hbm),
         scratch_shapes=[
+            pltpu.SMEM((links, tiles), i32),
+            pltpu.SMEM((links, tiles), i32),
+            pltpu.VMEM((CAP, devices, padded), i32),
             pltpu.VMEM((comps, rows + 2 * wide, levels, lanes), f32),
             pltpu.VMEM((comps, rows, levels, lanes), i32),
             pltpu.VMEM((comps, rows, levels, lanes), i32),
@@ -827,22 +815,18 @@
             pltpu.VMEM((4, rows, levels, lanes), f32),
             pltpu.VMEM((rows, levels, lanes), i32),
             pltpu.VMEM((rows, levels, chans, lanes), f32),
-            dma((levels,)),
-            dma((chans,)),
-            dma((levels,)),
-            dma((levels,)),
+            dma((8,)),
+            dma(()),
+            dma(()),
+            dma((16,)),
+            dma((16,)),
+            dma((2,)),
+            dma((2,)),
+            dma((3,)),
+            dma((2,)),
             dma((2,)),
             dma(()),
-            dma((rows // 2,)),
-            dma((16,)),
-            dma((16,)),
-            dma((devices,)),
-            dma((devices,)),
-            dma((devices,)),
-            dma((devices,)),
-            dma((near,)),
-            dma((near,)),
-            dma((2,)),
+            dma((3,)),
             dma(()),
         ],
         compiler_params=pltpu.CompilerParams(
@@ -853,18 +837,17 @@
     return pl.pallas_call(
         functools.partial(join_kernel, (chans, levels, rows, blocks, direct, cells)),
         out_shape=jax.ShapeDtypeStruct((chans, levels, rows, lanes), f32),
-        in_specs=[hbm, hbm, smem, hbm],
+        in_specs=[hbm] * 4,
         out_specs=hbm,
         scratch_shapes=[
+            pltpu.SMEM((CAP, devices, padded), i32),
+            pltpu.VMEM((rows, chans, levels, lanes), f32),
             pltpu.VMEM((blocks + 1, chans, levels, lanes), f32),
             pltpu.VMEM((blocks + 1, chans, levels, lanes), f32),
             pltpu.VMEM((near, CAP, depth, cols), b16),
             pltpu.VMEM((near, CAP, direct, cols), b16),
             pltpu.VMEM((blocks, depth - direct, cols), jnp.int16),
-            dma((levels,)),
-            dma(()),
-            dma(()),
-            dma(()),
+            dma((5,)),
             dma((rows,)),
         ],
         compiler_params=pltpu.CompilerParams(vmem_limit_bytes=62 * 1024 * 1024),

time: 58.2 us -> 53.1 us (0.912)
  Pallas kernels: 58 us -> 53 us
    pallas_call x1, Pallas kernels: 53.3 us -> 50 us  [body(): pl.pallas_call(functools.partial(step_kernel, dims), out_shape=(jax.Shape...]
    pallas_call x1, Pallas kernels: 4.66 us -> 2.98 us  [body(): pl.pallas_call(functools.partial(join_kernel, (chans, levels, rows, block...]
where the time goes in v4:
time: 53.1 us; the launch traced here: 53 us
  Pallas kernels  53 us (100%)
    pallas_call x1, Pallas kernels, body(): pl.pallas_call(functools.partial(step_kernel, dims), out_shape=(jax.Shape...  50 us
    pallas_call x1, Pallas kernels, body(): pl.pallas_call(functools.partial(join_kernel, (chans, levels, rows, block...  2.98 us

profile of v4, /device:TPU:0, one launch (start us, length us, event | category | flops | bytes accessed | tf_op | source)
XLA Modules:
  0.0 53.0 jit_solution(9238243308863140353)
XLA Ops:
  0.0 50.0 %step.1 = (f32[16,8,16,128]{3,2,1,0:T(8,128)}, bf16[32,2,128,128]{3,2,1,0:T(8,128)(2,1)}, s32[2,32,128]{2,1,0:T(8,128)}, s16[16,80,128]{2,1,0:T(8,128)(2,1)}) custom-call(f32[3,8,16,128]{3,2,1,0:T(8,128)} %winds_hbm.1, s32[3,8,16,128]{3,2,1,0:T(8,128)} %first_hbm.1, s32[3,8,16,128]{3,2,1,0:T(8,128)} %second_hbm.1, f32[16,8,16,128]{3,2,1,0:T(8,128)} %tracers_hbm.1, ...), custom_call_target="tpu_custom_call" | custom-call | tf_op jit(solution)/shard_map/step/pallas_call | solution.py:772
  50.0 3.0 %join.1 = f32[16,8,16,128]{3,2,1,0:T(8,128)} custom-call(f32[16,8,16,128]{3,2,1,0:T(8,128)} %get-tuple-element.9.moved_hbm, bf16[32,2,128,128]{3,2,1,0:T(8,128)(2,1)} %get-tuple-element.10.arrived_hbm, s32[2,32,128]{2,1,0:T(8,128)} %get-tuple-element.11.labels_hbm, s16[16,80,128]{2,1,0:T(8,128)(2,1)} %get-tuple-element.12.dense_hbm), custom_call_target="tpu_custom_call" | custom-call | tf_op jit(solution)/shard_map/join/pallas_call | solution.py:837

commit v5 on v4

--- a/solution.py
+++ b/solution.py
@@ -17,6 +17,9 @@
 CODES = 32767.0
 ITEM_LOW = 0.049804688 * 0.00019931793
 ITEM_HIGH = 5.0 * 0.019897461
+TRACER_LEAST = 6.0 * 2.0**-24
+TRACER_LOW = math.log(TRACER_LEAST)
+TRACER_SCALE = (CODES - 1.0) / (math.log(6.0) - TRACER_LOW)
 
 
 def cubic_weights(frac):
@@ -51,6 +54,20 @@
     return spread
 
 
+def to_code(value):
+    size = jnp.abs(value)
+    code = jnp.clip(jnp.round((jnp.log(size) - TRACER_LOW) * TRACER_SCALE), 0.0, CODES - 1.0) + 1.0
+    code = jnp.where(size < TRACER_LEAST, 0.0, code)
+    return jnp.where(value < 0.0, -code, code).astype(jnp.int32).astype(jnp.int16)
+
+
+def from_code(code):
+    code = code.astype(jnp.int32).astype(jnp.float32)
+    size = jnp.exp((jnp.abs(code) - 1.0) * (1.0 / TRACER_SCALE) + TRACER_LOW)
+    size = jnp.where(code == 0.0, 0.0, size)
+    return jnp.where(code < 0.0, -size, size)
+
+
 def code_range(cells, count):
     low = math.log(0.98 * cells * ITEM_LOW)
     high = math.log(1.02 * cells * ITEM_HIGH * count)
@@ -64,7 +81,7 @@
     owner_ref, block_ref, labels_ref,
     wind_pad, first_v, second_v, tracer_pad, fluxes_v, weights_v,
     products, outgoing, codes_v, codes_s, marks_v, relayed, running, dense_v, table_v, table_s,
-    wind_pack, tracer_pack, wind_edge, tracer_edge,
+    wind_pack, tracer_pack, wind_edge, tracer_edge, codes_out, codes_in,
     shifted, lhs, rhs_a, rhs_b, masks, wind_w, wind_sum, lev_w, row_w, col_w, col_at, moved_v,
     load_sem, code_sem, moved_sem, halo_send, halo_recv, near_sem, far_sem, mark_sem, relay_sem,
     dense_sem, table_sem, own_sem, labels_sem,
@@ -154,12 +171,12 @@
         halo(9, tracer_pack, tracer_edge.at[1, pl.ds(narrow, rows)], (lat, west)),
     ]
     tracer_north = [
-        halo(10, tracer_pad.at[:, pl.ds(narrow, narrow)], tracer_pad.at[:, below_rows], (north, lon)),
+        halo(10, codes_out.at[0], codes_in.at[1], (north, lon)),
         halo(11, tracer_pack.at[first_rows], tracer_edge.at[0, below_rows], (north, east)),
         halo(12, tracer_pack.at[first_rows], tracer_edge.at[1, below_rows], (north, west)),
     ]
     tracer_south = [
-        halo(13, tracer_pad.at[:, pl.ds(rows, narrow)], tracer_pad.at[:, above_rows], (south, lon)),
+        halo(13, codes_out.at[1], codes_in.at[0], (south, lon)),
         halo(14, tracer_pack.at[last_rows], tracer_edge.at[0, above_rows], (south, east)),
         halo(15, tracer_pack.at[last_rows], tracer_edge.at[1, above_rows], (south, west)),
     ]
@@ -172,10 +189,20 @@
 
     start, arrive, leave = (lambda c: c.start()), (lambda c: c.wait_recv()), (lambda c: c.wait_send())
     whole(inner_winds, load_sem.at[2]).wait()
+    pl.semaphore_wait(barrier, devices - 1)
+    each(has_north, wind_north[:1], start)
+    each(has_south, wind_south[:1], start)
     whole(inner_tracers, load_sem.at[3]).wait()
-    pl.semaphore_wait(barrier, devices - 1)
-    each(has_north, [wind_north[0], tracer_north[0]], start)
-    each(has_south, [wind_south[0], tracer_south[0]], start)
+
+    def encode_rows(level, carry):
+        for side, first in ((0, narrow), (1, rows)):
+            for r in range(narrow):
+                codes_out[side, level, r] = to_code(tracer_pad[level, first + r])
+        return carry
+
+    lax.fori_loop(0, levels, encode_rows, 0)
+    each(has_north, tracer_north[:1], start)
+    each(has_south, tracer_south[:1], start)
 
     for half in range(halves):
         for comp in range(comps):
@@ -546,6 +573,17 @@
         copy.wait_recv()
     each(has_north, tracer_south, arrive)
     each(has_south, tracer_north, arrive)
+
+    def decode_rows(place, first):
+        def decode_level(level, carry):
+            for r in range(narrow):
+                tracer_pad[level, first + r] = from_code(codes_in[place, level, r])
+            return carry
+
+        lax.fori_loop(0, levels, decode_level, 0)
+
+    pl.when(has_north)(functools.partial(decode_rows, 0, 0))
+    pl.when(has_south)(functools.partial(decode_rows, 1, narrow + rows))
 
     def split_row(r, carry):
         merged = jnp.where(lane16 % 16 < 8, tracer_edge[0, r], tracer_edge[1, r])
@@ -803,6 +841,8 @@
             pltpu.VMEM((rows, chans, lanes), f32),
             pltpu.VMEM((2, halves + 2, comps, levels, lanes), f32),
             pltpu.VMEM((2, rows + 2 * narrow, chans, lanes), f32),
+            pltpu.VMEM((2, levels, narrow, chans, lanes), jnp.int16),
+            pltpu.VMEM((2, levels, narrow, chans, lanes), jnp.int16),
             pltpu.VMEM((5 * (2 * wide + 1), comps, rows + 2 * wide, levels, lanes), f32),
             pltpu.VMEM((levels, rows + 2 * narrow, chans, 3 * lanes), b16),
             pltpu.VMEM((4 * lanes, 2 * lanes), b16),

time: 53.1 us -> 51 us (0.960)
  Pallas kernels: 53 us -> 50.9 us
    pallas_call x1, Pallas kernels: 50 us -> 47.9 us  [body(): pl.pallas_call(functools.partial(step_kernel, dims), out_shape=(jax.Shape...]
where the time goes in v5:
time: 51 us; the launch traced here: 50.9 us
  Pallas kernels  50.9 us (100%)
    pallas_call x1, Pallas kernels, body(): pl.pallas_call(functools.partial(step_kernel, dims), out_shape=(jax.Shape...  47.9 us
    pallas_call x1, Pallas kernels, body(): pl.pallas_call(functools.partial(join_kernel, (chans, levels, rows, block...  2.98 us

profile of v5, /device:TPU:0, one launch (start us, length us, event | category | flops | bytes accessed | tf_op | source)
XLA Modules:
  0.0 50.9 jit_solution(3848657494498150134)
XLA Ops:
  0.0 47.9 %step.1 = (f32[16,8,16,128]{3,2,1,0:T(8,128)}, bf16[32,2,128,128]{3,2,1,0:T(8,128)(2,1)}, s32[2,32,128]{2,1,0:T(8,128)}, s16[16,80,128]{2,1,0:T(8,128)(2,1)}) custom-call(f32[3,8,16,128]{3,2,1,0:T(8,128)} %winds_hbm.1, s32[3,8,16,128]{3,2,1,0:T(8,128)} %first_hbm.1, s32[3,8,16,128]{3,2,1,0:T(8,128)} %second_hbm.1, f32[16,8,16,128]{3,2,1,0:T(8,128)} %tracers_hbm.1, ...), custom_call_target="tpu_custom_call" | custom-call | tf_op jit(solution)/shard_map/step/pallas_call | solution.py:810
  47.9 3.0 %join.1 = f32[16,8,16,128]{3,2,1,0:T(8,128)} custom-call(f32[16,8,16,128]{3,2,1,0:T(8,128)} %get-tuple-element.9.moved_hbm, bf16[32,2,128,128]{3,2,1,0:T(8,128)(2,1)} %get-tuple-element.10.arrived_hbm, s32[2,32,128]{2,1,0:T(8,128)} %get-tuple-element.11.labels_hbm, s16[16,80,128]{2,1,0:T(8,128)(2,1)} %get-tuple-element.12.dense_hbm), custom_call_target="tpu_custom_call" | custom-call | tf_op jit(solution)/shard_map/join/pallas_call | solution.py:877

commit v6 on v5

--- a/solution.py
+++ b/solution.py
@@ -17,6 +17,7 @@
 CODES = 32767.0
 ITEM_LOW = 0.049804688 * 0.00019931793
 ITEM_HIGH = 5.0 * 0.019897461
+WIND_MOST = 4.0
 TRACER_LEAST = 6.0 * 2.0**-24
 TRACER_LOW = math.log(TRACER_LEAST)
 TRACER_SCALE = (CODES - 1.0) / (math.log(6.0) - TRACER_LOW)
@@ -61,6 +62,14 @@
     return jnp.where(value < 0.0, -code, code).astype(jnp.int32).astype(jnp.int16)
 
 
+def to_fixed(wind):
+    return jnp.round(wind * (CODES / WIND_MOST)).astype(jnp.int32).astype(jnp.int16)
+
+
+def from_fixed(code):
+    return code.astype(jnp.int32).astype(jnp.float32) * (WIND_MOST / CODES)
+
+
 def from_code(code):
     code = code.astype(jnp.int32).astype(jnp.float32)
     size = jnp.exp((jnp.abs(code) - 1.0) * (1.0 / TRACER_SCALE) + TRACER_LOW)
@@ -82,6 +91,7 @@
     wind_pad, first_v, second_v, tracer_pad, fluxes_v, weights_v,
     products, outgoing, codes_v, codes_s, marks_v, relayed, running, dense_v, table_v, table_s,
     wind_pack, tracer_pack, wind_edge, tracer_edge, codes_out, codes_in,
+    pack_out, pack_in, wind_out, wind_in,
     shifted, lhs, rhs_a, rhs_b, masks, wind_w, wind_sum, lev_w, row_w, col_w, col_at, moved_v,
     load_sem, code_sem, moved_sem, halo_send, halo_recv, near_sem, far_sem, mark_sem, relay_sem,
     dense_sem, table_sem, own_sem, labels_sem,
@@ -155,30 +165,28 @@
         halo(1, wind_pack, wind_edge.at[1, pl.ds(1, halves)], (lat, west)),
     ]
     wind_north = [
-        halo(2, wind_pad.at[:, pl.ds(wide, wide)], wind_pad.at[:, pl.ds(wide + rows, wide)], (north, lon)),
+        halo(2, wind_out.at[0], wind_in.at[1], (north, lon)),
         halo(3, wind_pack.at[0], wind_edge.at[0, halves + 1], (north, east)),
         halo(4, wind_pack.at[0], wind_edge.at[1, halves + 1], (north, west)),
     ]
     wind_south = [
-        halo(5, wind_pad.at[:, pl.ds(rows, wide)], wind_pad.at[:, pl.ds(0, wide)], (south, lon)),
+        halo(5, wind_out.at[1], wind_in.at[0], (south, lon)),
         halo(6, wind_pack.at[halves - 1], wind_edge.at[0, 0], (south, east)),
         halo(7, wind_pack.at[halves - 1], wind_edge.at[1, 0], (south, west)),
     ]
-    first_rows, last_rows = pl.ds(0, narrow), pl.ds(rows - narrow, narrow)
-    above_rows, below_rows = pl.ds(0, narrow), pl.ds(narrow + rows, narrow)
     tracer_sides = [
         halo(8, tracer_pack, tracer_edge.at[0, pl.ds(narrow, rows)], (lat, east)),
         halo(9, tracer_pack, tracer_edge.at[1, pl.ds(narrow, rows)], (lat, west)),
     ]
     tracer_north = [
         halo(10, codes_out.at[0], codes_in.at[1], (north, lon)),
-        halo(11, tracer_pack.at[first_rows], tracer_edge.at[0, below_rows], (north, east)),
-        halo(12, tracer_pack.at[first_rows], tracer_edge.at[1, below_rows], (north, west)),
+        halo(11, pack_out.at[0], pack_in.at[1, 0], (north, east)),
+        halo(12, pack_out.at[0], pack_in.at[1, 1], (north, west)),
     ]
     tracer_south = [
         halo(13, codes_out.at[1], codes_in.at[0], (south, lon)),
-        halo(14, tracer_pack.at[last_rows], tracer_edge.at[0, above_rows], (south, east)),
-        halo(15, tracer_pack.at[last_rows], tracer_edge.at[1, above_rows], (south, west)),
+        halo(14, pack_out.at[1], pack_in.at[0, 0], (south, east)),
+        halo(15, pack_out.at[1], pack_in.at[0, 1], (south, west)),
     ]
 
     def each(condition, copies, act):
@@ -189,6 +197,10 @@
 
     start, arrive, leave = (lambda c: c.start()), (lambda c: c.wait_recv()), (lambda c: c.wait_send())
     whole(inner_winds, load_sem.at[2]).wait()
+    for side, first in ((0, wide), (1, rows)):
+        for comp in range(comps):
+            for r in range(wide):
+                wind_out[side, comp, r] = to_fixed(wind_pad[comp, first + r])
     pl.semaphore_wait(barrier, devices - 1)
     each(has_north, wind_north[:1], start)
     each(has_south, wind_south[:1], start)
@@ -212,7 +224,7 @@
                 packed = jnp.where(
                     lane8 // 16 == p, pltpu.roll(value, (16 * p + 8) % lanes, 1), packed
                 )
-            wind_pack[half, comp] = packed
+            wind_pack[half, comp] = to_fixed(packed)
 
     each(has_north, wind_north[1:], start)
     each(has_south, wind_south[1:], start)
@@ -232,6 +244,9 @@
 
     lax.fori_loop(0, rows // 2, pack_row, 0)
 
+    for r in range(narrow):
+        pack_out[0, r] = to_code(tracer_pack[r])
+        pack_out[1, r] = to_code(tracer_pack[rows - narrow + r])
     each(has_north, tracer_north[1:], start)
     each(has_south, tracer_south[1:], start)
     for copy in tracer_sides:
@@ -267,14 +282,14 @@
     @pl.when(jnp.logical_not(has_north))
     def _():
         wind_pad[:, 0:wide] = jnp.zeros((comps, wide, levels, lanes), jnp.float32)
-        wind_edge[:, 0] = jnp.zeros((2, comps, levels, lanes), jnp.float32)
+        wind_edge[:, 0] = jnp.zeros((2, comps, levels, lanes), jnp.int16)
         tracer_pad[:, 0:narrow] = jnp.zeros((levels, narrow, chans, lanes), jnp.float32)
         tracer_edge[:, 0:narrow] = jnp.zeros((2, narrow, chans, lanes), jnp.float32)
 
     @pl.when(jnp.logical_not(has_south))
     def _():
         wind_pad[:, wide + rows :] = jnp.zeros((comps, wide, levels, lanes), jnp.float32)
-        wind_edge[:, halves + 1] = jnp.zeros((2, comps, levels, lanes), jnp.float32)
+        wind_edge[:, halves + 1] = jnp.zeros((2, comps, levels, lanes), jnp.int16)
         tracer_pad[:, narrow + rows :] = jnp.zeros((levels, narrow, chans, lanes), jnp.float32)
         tracer_edge[:, narrow + rows :] = jnp.zeros((2, narrow, chans, lanes), jnp.float32)
 
@@ -479,12 +494,22 @@
     each(has_north, wind_south, arrive)
     each(has_south, wind_north, arrive)
 
+    def wind_rows_in(place, first):
+        for comp in range(comps):
+            for r in range(wide):
+                wind_pad[comp, first + r] = from_fixed(wind_in[place, comp, r])
+
+    pl.when(has_north)(functools.partial(wind_rows_in, 0, 0))
+    pl.when(has_south)(functools.partial(wind_rows_in, 1, wide + rows))
+
     def shift_row(r, carry):
         turned = r + 8 - wide
         half, p = turned // 8, turned % 8
         back = lax.rem(2 * lanes - 8 - 16 * p, lanes)
         for comp in range(comps):
-            merged = jnp.where(lane8 % 16 < 8, wind_edge[0, half, comp], wind_edge[1, half, comp])
+            merged = jnp.where(
+                lane8 % 16 < 8, from_fixed(wind_edge[0, half, comp]), from_fixed(wind_edge[1, half, comp])
+            )
             edge = pltpu.roll(merged, back, 1)
             main = wind_pad[comp, r]
             for e in range(taps):
@@ -581,6 +606,9 @@
             return carry
 
         lax.fori_loop(0, levels, decode_level, 0)
+        for side in range(2):
+            for r in range(narrow):
+                tracer_edge[side, first + r] = from_code(pack_in[place, side, r])
 
     pl.when(has_north)(functools.partial(decode_rows, 0, 0))
     pl.when(has_south)(functools.partial(decode_rows, 1, narrow + rows))
@@ -837,12 +865,16 @@
             pltpu.VMEM((blocks, depth - direct, cols), jnp.int16),
             pltpu.VMEM((near * CAP, padded), i32),
             pltpu.SMEM((near * CAP, padded), i32),
-            pltpu.VMEM((halves, comps, levels, lanes), f32),
+            pltpu.VMEM((halves, comps, levels, lanes), jnp.int16),
             pltpu.VMEM((rows, chans, lanes), f32),
-            pltpu.VMEM((2, halves + 2, comps, levels, lanes), f32),
+            pltpu.VMEM((2, halves + 2, comps, levels, lanes), jnp.int16),
             pltpu.VMEM((2, rows + 2 * narrow, chans, lanes), f32),
             pltpu.VMEM((2, levels, narrow, chans, lanes), jnp.int16),
             pltpu.VMEM((2, levels, narrow, chans, lanes), jnp.int16),
+            pltpu.VMEM((2, narrow, chans, lanes), jnp.int16),
+            pltpu.VMEM((2, 2, narrow, chans, lanes), jnp.int16),
+            pltpu.VMEM((2, comps, wide, levels, lanes), jnp.int16),
+            pltpu.VMEM((2, comps, wide, levels, lanes), jnp.int16),
             pltpu.VMEM((5 * (2 * wide + 1), comps, rows + 2 * wide, levels, lanes), f32),
             pltpu.VMEM((levels, rows + 2 * narrow, chans, 3 * lanes), b16),
             pltpu.VMEM((4 * lanes, 2 * lanes), b16),

time: 51 us -> 50 us (0.980)
  Pallas kernels: 50.9 us -> 49.8 us
    pallas_call x1, Pallas kernels: 47.9 us -> 46.9 us  [body(): pl.pallas_call(functools.partial(step_kernel, dims), out_shape=(jax.Shape...]
where the time goes in v6:
time: 50 us; the launch traced here: 49.8 us
  Pallas kernels  49.8 us (100%)
    pallas_call x1, Pallas kernels, body(): pl.pallas_call(functools.partial(step_kernel, dims), out_shape=(jax.Shape...  46.9 us
    pallas_call x1, Pallas kernels, body(): pl.pallas_call(functools.partial(join_kernel, (chans, levels, rows, block...  2.98 us

profile of v6, /device:TPU:0, one launch (start us, length us, event | category | flops | bytes accessed | tf_op | source)
XLA Modules:
  0.0 49.8 jit_solution(1189236950831420168)
XLA Ops:
  0.0 46.9 %step.1 = (f32[16,8,16,128]{3,2,1,0:T(8,128)}, bf16[32,2,128,128]{3,2,1,0:T(8,128)(2,1)}, s32[2,32,128]{2,1,0:T(8,128)}, s16[16,80,128]{2,1,0:T(8,128)(2,1)}) custom-call(f32[3,8,16,128]{3,2,1,0:T(8,128)} %winds_hbm.1, s32[3,8,16,128]{3,2,1,0:T(8,128)} %first_hbm.1, s32[3,8,16,128]{3,2,1,0:T(8,128)} %second_hbm.1, f32[16,8,16,128]{3,2,1,0:T(8,128)} %tracers_hbm.1, ...), custom_call_target="tpu_custom_call" | custom-call | tf_op jit(solution)/shard_map/step/pallas_call | solution.py:838
  46.9 3.0 %join.1 = f32[16,8,16,128]{3,2,1,0:T(8,128)} custom-call(f32[16,8,16,128]{3,2,1,0:T(8,128)} %get-tuple-element.9.moved_hbm, bf16[32,2,128,128]{3,2,1,0:T(8,128)(2,1)} %get-tuple-element.10.arrived_hbm, s32[2,32,128]{2,1,0:T(8,128)} %get-tuple-element.11.labels_hbm, s16[16,80,128]{2,1,0:T(8,128)(2,1)} %get-tuple-element.12.dense_hbm), custom_call_target="tpu_custom_call" | custom-call | tf_op jit(solution)/shard_map/join/pallas_call | solution.py:909

commit v7 on v6

--- a/solution.py
+++ b/solution.py
@@ -717,9 +717,10 @@
 
         pl.when(pair == 1)(sort_relayed)
         pl.when(pair == 2)(sum_relayed)
-        pl.when(pair == 3)(dense_copy.start)
         pl.when(pair == pairs - 1)(take_labels)
         for level in range(levels):
+            if level == 4:
+                pl.when(pair == 2)(dense_copy.start)
             pl.when(pair >= 0)(functools.partial(level_step, level))
         moved_copy(pair).start()
         return carry

time: 50 us -> 50 us (level)
  no operation moved by 1% of the time
where the time goes in v7:
time: 50 us; the launch traced here: 49.8 us
  Pallas kernels  49.8 us (100%)
    pallas_call x1, Pallas kernels, body(): pl.pallas_call(functools.partial(step_kernel, dims), out_shape=(jax.Shape...  46.9 us
    pallas_call x1, Pallas kernels, body(): pl.pallas_call(functools.partial(join_kernel, (chans, levels, rows, block...  2.98 us

profile of v7, /device:TPU:0, one launch (start us, length us, event | category | flops | bytes accessed | tf_op | source)
XLA Modules:
  0.0 49.8 jit_solution(16594388880361298439)
XLA Ops:
  0.0 46.9 %step.1 = (f32[16,8,16,128]{3,2,1,0:T(8,128)}, bf16[32,2,128,128]{3,2,1,0:T(8,128)(2,1)}, s32[2,32,128]{2,1,0:T(8,128)}, s16[16,80,128]{2,1,0:T(8,128)(2,1)}) custom-call(f32[3,8,16,128]{3,2,1,0:T(8,128)} %winds_hbm.1, s32[3,8,16,128]{3,2,1,0:T(8,128)} %first_hbm.1, s32[3,8,16,128]{3,2,1,0:T(8,128)} %second_hbm.1, f32[16,8,16,128]{3,2,1,0:T(8,128)} %tracers_hbm.1, ...), custom_call_target="tpu_custom_call" | custom-call | tf_op jit(solution)/shard_map/step/pallas_call | solution.py:839
  46.9 3.0 %join.1 = f32[16,8,16,128]{3,2,1,0:T(8,128)} custom-call(f32[16,8,16,128]{3,2,1,0:T(8,128)} %get-tuple-element.9.moved_hbm, bf16[32,2,128,128]{3,2,1,0:T(8,128)(2,1)} %get-tuple-element.10.arrived_hbm, s32[2,32,128]{2,1,0:T(8,128)} %get-tuple-element.11.labels_hbm, s16[16,80,128]{2,1,0:T(8,128)(2,1)} %get-tuple-element.12.dense_hbm), custom_call_target="tpu_custom_call" | custom-call | tf_op jit(solution)/shard_map/join/pallas_call | solution.py:910
